TPU v7x, 32 devices: a whole 2x2x4 slice. The times are simulated.
32 devices in a mesh: gx: 2 (over core), gy: 4 (over y, x), gz: 4 (over z).
Axes of the slice: x: 2, y: 2, z: 4, core: 2. Of those that a mesh axis runs over, the one named last changes fastest.
Arguments:
- basis: float32 [32, 262144], P(None, ('gx', 'gy', 'gz')), may hold values from -5.5 to 5.5
- sigma: float32 [32], replicated, may hold values from 1 to 8
- snapshots: float32 [64, 262144], P(None, ('gx', 'gy', 'gz')), may hold values from -200 to 200
Outputs:
- modes: float32 [32, 262144], P(None, ('gx', 'gy', 'gz'))
- values: float32 [32], replicated
All inputs are finite; a program needn't handle non-finite values.
Results may differ from a plain program's by a relative error of at most 0.00016.
Values sent between devices are 32-bit elements; how exact they have to be, the bound alone decides.
No kernel may reach another device: no remote copies, remote signals or barrier semaphores. Data moves between devices by JAX's collectives and lax.ppermute only.
A program may use at most 64 MiB of HBM per device.

v0:
```python
import jax
import jax.numpy as jnp
from jax import lax
from jax.sharding import PartitionSpec as P

ITERS = 4


HIGH = lax.Precision.HIGHEST


def inner(left, right, total):
    product = lax.dot_general(
        left, right, (((1,), (1,)), ((), ())), precision=HIGH, preferred_element_type=jnp.float32
    )
    return product / total


def remove(block, coeffs, basis):
    return block - jnp.dot(coeffs.T, basis, precision=HIGH)


def orthonormal(block):
    for repeat in range(2):
        factor = jnp.linalg.cholesky(jnp.dot(block.T, block, precision=HIGH))
        block = jax.scipy.linalg.solve_triangular(factor, block.T, lower=True).T
    return block


def rotate(sigma, coeffs, factor):
    modes_count = sigma.shape[0]
    fresh_count = factor.shape[0]
    upper_rows = jnp.concatenate([jnp.diag(sigma), coeffs], axis=1)
    lower_rows = jnp.concatenate(
        [jnp.zeros((fresh_count, modes_count), jnp.float32), factor], axis=1
    )
    core = jnp.concatenate([upper_rows, lower_rows], axis=0)
    square = jnp.dot(core, core.T, precision=HIGH)
    frame = jnp.eye(modes_count + fresh_count, modes_count, dtype=jnp.float32)
    for step in range(ITERS):
        frame = orthonormal(jnp.dot(square, frame, precision=HIGH))
    ritz = jnp.sum(frame * jnp.dot(square, frame, precision=HIGH), axis=0)
    return (frame, jnp.sqrt(ritz))


def per_device(basis, sigma, snapshots):
    modes_count = basis.shape[0]
    total = basis.shape[1] * lax.axis_size(("gx", "gy", "gz")) * 1.0
    correlation, first, snap_gram = lax.psum(
        (
            inner(basis, basis, total),
            inner(basis, snapshots, total),
            inner(snapshots, snapshots, total),
        ),
        ("gx", "gy", "gz"),
    )
    second = first - jnp.dot(correlation, first, precision=HIGH)
    partial_value = remove(snapshots, first, basis)
    residual = remove(partial_value, second, basis)
    joined = first + second
    cross = jnp.dot(joined.T, first, precision=HIGH)
    bent = jnp.dot(joined.T, jnp.dot(correlation, joined, precision=HIGH), precision=HIGH)
    lower = jnp.linalg.cholesky(snap_gram - cross - cross.T + bent)
    fresh = jax.scipy.linalg.solve_triangular(lower, residual, lower=True)
    frame, values = rotate(sigma, first + second, lower.T)
    modes = jnp.dot(frame[:modes_count].T, basis, precision=HIGH) + jnp.dot(
        frame[modes_count:].T, fresh, precision=HIGH
    )
    return (modes, values)


def solution(mesh):
    placed = (P(None, ("gx", "gy", "gz")), P(), P(None, ("gx", "gy", "gz")))
    return jax.shard_map(
        per_device,
        mesh=mesh,
        in_specs=placed,
        out_specs=(P(None, ("gx", "gy", "gz")), P()),
        check_vma=False,
    )
```

profile of v0, /device:TPU:0, one launch (start us, length us, event | category | flops | bytes accessed | tf_op | source)
XLA Modules:
  0.0 132.6 jit_solution(9067813681668639900)
XLA Ops:
  0.6 4.1 %convolution_multiply_fusion = f32[64,64]{0,1:T(8,128)S(1)} fusion(f32[64,8192]{1,0:T(8,128)} %param.8), kind=kOutput, calls=%fused_computation.4 | convolution fusion | flops 402657280 | bytes 2113536 | tf_op jit(solution)/shard_map/dot_general | solution.py:13
  4.8 1.0 convolution_multiply_fusion.2
  5.8 0.6 copy-done.1
  6.4 1.8 %convolution_multiply_fusion.3 = f32[32,64]{1,0:T(8,128)S(1)} fusion(f32[32,8192]{1,0:T(8,128)S(1)} %copy-done, f32[64,8192]{1,0:T(8,128)S(1)} %copy-done.1), kind=kOutput, calls=%fused_computation.8 | convolution fusion | flops 201328640 | bytes 3153920 | tf_op jit(solution)/shard_map/dot_general | solution.py:13
  8.2 42.8 %all-reduce.1 = (f32[32,64]{1,0:T(8,128)S(1)}, f32[32,32]{1,0:T(8,128)S(1)}, f32[64,64]{0,1:T(8,128)S(1)}) all-reduce(f32[32,64]{1,0:T(8,128)S(1)} %convolution_multiply_fusion.3, f32[32,32]{1,0:T(8,128)S(1)} %convolution_multiply_fusion.2, ...), channel_id=1, replica_groups=mesh['gx'=2,'gy'=4,'gz'=4] {'gx','gy','gz'}, use_global_device_ids=true, to_apply=%region_0.0 | all-reduce | flops 7168 | bytes 57344 | tf_op jit(solution)/shard_map/psum | solution.py:49
  51.1 0.2 fusion.69
  51.5 0.3 convolution_add_fusion.1
  51.9 5.8 %cholesky.34 = f32[64,64]{1,0:T(8,128)S(1)} custom-call(f32[64,64]{1,0:T(8,128)S(1)} %fusion.7), custom_call_target="Cholesky" | custom-call | tf_op jit(solution)/shard_map/jit(cholesky)/cholesky | solution.py:63
  57.8 0.6 compare_reduce_fusion.8
  58.4 0.7 select_bitcast_fusion
  59.1 4.9 %custom-call.12 = f32[1,64,64]{1,2,0:T(8,128)S(1)} custom-call(f32[1,64,64]{2,1,0:T(8,128)S(1)} %get-tuple-element.7), custom_call_target="InvertDiagBlocksLowerTriangular" | custom-call | tf_op jit(solution)/shard_map/jit(_solve_triangular)/triangular_solve | solution.py:64
  64.0 1.9 %convolution_subtract_fusion.1 = f32[64,8192]{1,0:T(8,128)S(1)} fusion(f32[64,8192]{1,0:T(8,128)S(1)} %copy-done.1, f32[32,64]{1,0:T(8,128)S(1)} %get-tuple-element.4, f32[32,8192]{1,0:T(8,128)S(1)} %copy-done), kind=kOutput, calls=%fused_computation.1 | convolution fusion | flops 201850880 | bytes 5251072 | tf_op jit(solution)/shard_map/dot_general | solution.py:20
  65.9 1.9 %convolution_subtract_fusion = f32[64,8192]{1,0:T(8,128)S(1)} fusion(f32[64,8192]{1,0:T(8,128)S(1)} %convolution_subtract_fusion.1, f32[32,64]{1,0:T(8,128)S(1)} %get-tuple-element.10, f32[32,8192]{1,0:T(8,128)S(1)} %copy-done), kind=kOutput, calls=%fused_computation | convolution fusion | flops 201850880 | bytes 5251072 | tf_op jit(solution)/shard_map/dot_general | solution.py:20
  67.8 1.9 %fusion.5 = f32[64,8192]{1,0:T(8,128)S(1)} fusion(f32[64,8192]{1,0:T(8,128)S(1)} %convolution_subtract_fusion, f32[1,64,64]{1,2,0:T(8,128)S(1)} %custom-call.12), kind=kOutput, calls=%fused_computation.17 | convolution fusion | flops 402653184 | bytes 4210688 | tf_op jit(solution)/shard_map/jit(_solve_triangular)/triangular_solve | solution.py:64
  69.9 0.3 fusion.1
  70.3 0.2 fusion.4
  70.7 2.9 %cholesky.172 = f32[32,32]{1,0:T(8,128)S(1)} custom-call(f32[32,32]{1,0:T(8,128)S(1)} %fusion.49), custom_call_target="Cholesky" | custom-call | tf_op jit(solution)/shard_map/jit(cholesky)/cholesky | solution.py:25
  73.7 0.6 compare_reduce_fusion.7
  74.3 0.7 fusion.11
  75.0 2.4 %custom-call.20 = f32[1,32,32]{1,2,0:T(8,128)S(1)} custom-call(f32[1,32,32]{2,1,0:T(8,128)S(1)} %fusion.11), custom_call_target="InvertDiagBlocksLowerTriangular" | custom-call | tf_op jit(solution)/shard_map/jit(_solve_triangular)/triangular_solve | solution.py:26
  77.4 0.2 fusion.46
  77.9 2.9 %cholesky.183 = f32[32,32]{1,0:T(8,128)S(1)} custom-call(f32[32,32]{1,0:T(8,128)S(1)} %fusion.45), custom_call_target="Cholesky" | custom-call | tf_op jit(solution)/shard_map/jit(cholesky)/cholesky | solution.py:25
  80.9 0.6 compare_reduce_fusion.6
  81.5 0.7 fusion.12
  82.2 2.4 %custom-call.21 = f32[1,32,32]{1,2,0:T(8,128)S(1)} custom-call(f32[1,32,32]{2,1,0:T(8,128)S(1)} %fusion.12), custom_call_target="InvertDiagBlocksLowerTriangular" | custom-call | tf_op jit(solution)/shard_map/jit(_solve_triangular)/triangular_solve | solution.py:26
  84.6 0.2 fusion.43
  84.8 0.2 fusion.73
  85.0 0.2 fusion.74
  85.3 2.9 %cholesky.194 = f32[32,32]{1,0:T(8,128)S(1)} custom-call(f32[32,32]{1,0:T(8,128)S(1)} %fusion.42), custom_call_target="Cholesky" | custom-call | tf_op jit(solution)/shard_map/jit(cholesky)/cholesky | solution.py:25
  88.2 0.6 compare_reduce_fusion.5
  88.9 0.7 fusion.13
  89.5 2.4 %custom-call.22 = f32[1,32,32]{1,2,0:T(8,128)S(1)} custom-call(f32[1,32,32]{2,1,0:T(8,128)S(1)} %fusion.13), custom_call_target="InvertDiagBlocksLowerTriangular" | custom-call | tf_op jit(solution)/shard_map/jit(_solve_triangular)/triangular_solve | solution.py:26
  92.0 0.2 fusion.39
  92.5 2.9 %cholesky.205 = f32[32,32]{1,0:T(8,128)S(1)} custom-call(f32[32,32]{1,0:T(8,128)S(1)} %fusion.38), custom_call_target="Cholesky" | custom-call | tf_op jit(solution)/shard_map/jit(cholesky)/cholesky | solution.py:25
  95.4 0.6 compare_reduce_fusion.4
  96.1 0.7 fusion.14
  96.7 2.4 %custom-call.23 = f32[1,32,32]{1,2,0:T(8,128)S(1)} custom-call(f32[1,32,32]{2,1,0:T(8,128)S(1)} %fusion.14), custom_call_target="InvertDiagBlocksLowerTriangular" | custom-call | tf_op jit(solution)/shard_map/jit(_solve_triangular)/triangular_solve | solution.py:26
  99.2 0.2 fusion.36
  99.4 0.2 fusion.76
  99.8 2.9 %cholesky.216 = f32[32,32]{1,0:T(8,128)S(1)} custom-call(f32[32,32]{1,0:T(8,128)S(1)} %fusion.35), custom_call_target="Cholesky" | custom-call | tf_op jit(solution)/shard_map/jit(cholesky)/cholesky | solution.py:25
  102.8 0.6 compare_reduce_fusion.3
  103.5 0.7 fusion.15
  104.1 2.4 %custom-call.24 = f32[1,32,32]{1,2,0:T(8,128)S(1)} custom-call(f32[1,32,32]{2,1,0:T(8,128)S(1)} %fusion.15), custom_call_target="InvertDiagBlocksLowerTriangular" | custom-call | tf_op jit(solution)/shard_map/jit(_solve_triangular)/triangular_solve | solution.py:26
  106.5 0.2 fusion.32
  107.0 2.9 %cholesky.227 = f32[32,32]{1,0:T(8,128)S(1)} custom-call(f32[32,32]{1,0:T(8,128)S(1)} %fusion.31), custom_call_target="Cholesky" | custom-call | tf_op jit(solution)/shard_map/jit(cholesky)/cholesky | solution.py:25
  110.0 0.6 compare_reduce_fusion.2
  110.6 0.7 fusion.16
  111.3 2.6 %custom-call.25 = f32[1,32,32]{1,2,0:T(8,128)S(1)} custom-call(f32[1,32,32]{2,1,0:T(8,128)S(1)} %fusion.16), custom_call_target="InvertDiagBlocksLowerTriangular" | custom-call | tf_op jit(solution)/shard_map/jit(_solve_triangular)/triangular_solve | solution.py:26
  113.8 0.2 fusion.29
  114.1 0.2 fusion.79
  114.5 2.9 %cholesky.238 = f32[32,32]{1,0:T(8,128)S(1)} custom-call(f32[32,32]{1,0:T(8,128)S(1)} %fusion.28), custom_call_target="Cholesky" | custom-call | tf_op jit(solution)/shard_map/jit(cholesky)/cholesky | solution.py:25
  117.5 0.6 compare_reduce_fusion.1
  118.1 0.7 fusion.17
  118.8 2.4 %custom-call.26 = f32[1,32,32]{1,2,0:T(8,128)S(1)} custom-call(f32[1,32,32]{2,1,0:T(8,128)S(1)} %fusion.17), custom_call_target="InvertDiagBlocksLowerTriangular" | custom-call | tf_op jit(solution)/shard_map/jit(_solve_triangular)/triangular_solve | solution.py:26
  121.2 0.2 fusion.25
  121.7 2.9 %cholesky.249 = f32[32,32]{1,0:T(8,128)S(1)} custom-call(f32[32,32]{1,0:T(8,128)S(1)} %fusion.24), custom_call_target="Cholesky" | custom-call | tf_op jit(solution)/shard_map/jit(cholesky)/cholesky | solution.py:25
  124.6 0.6 compare_reduce_fusion
  125.3 0.7 fusion.18
  125.9 2.4 %custom-call.27 = f32[1,32,32]{1,2,0:T(8,128)S(1)} custom-call(f32[1,32,32]{2,1,0:T(8,128)S(1)} %fusion.18), custom_call_target="InvertDiagBlocksLowerTriangular" | custom-call | tf_op jit(solution)/shard_map/jit(_solve_triangular)/triangular_solve | solution.py:26
  128.4 0.2 fusion.22
  128.6 1.0 fusion.20
  129.6 2.1 %convolution_add_fusion = f32[32,8192]{1,0:T(8,128)} fusion(f32[32,8192]{1,0:T(8,128)S(1)} %fusion.20, f32[64,8192]{1,0:T(8,128)S(1)} %fusion.5, f32[96,32]{0,1:T(8,128)S(1)} %bitcast.152), kind=kOutput, calls=%fused_computation.2 | convolution fusion | flops 201588736 | bytes 4206592 | tf_op jit(solution)/shard_map/dot_general | solution.py:66
  131.7 0.3 fusion
  132.0 0.5 sqrt.3
  (45 shorter events, 2.7 us)
Async XLA Ops:
  0.6 4.1 %copy-start = (f32[32,8192]{1,0:T(8,128)S(1)}, f32[32,8192]{1,0:T(8,128)}, u32[]{:S(2)}) copy-start(f32[32,8192]{1,0:T(8,128)} %param.6) | copy-start | bytes 3145732
  4.8 1.6 %copy-start.1 = (f32[64,8192]{1,0:T(8,128)S(1)}, f32[64,8192]{1,0:T(8,128)}, u32[]{:S(2)}) copy-start(f32[64,8192]{1,0:T(8,128)} %param.8) | copy-start | bytes 6291460
  67.8 1.9 %copy-start.2 = (f32[32]{0:T(128)S(1)}, f32[32]{0:T(128)}, u32[]{:S(2)}) copy-start(f32[32]{0:T(128)} %param.7) | copy-start | bytes 388
where the time goes:
time: 133 us
  other arithmetic  65.9 us (50%)
  blocking collectives  42.8 us (32%)
  matrix products  20.8 us (16%)
  local copies, waits for them, and re-layouts  1.98 us (1%)
    psum x1, blocking collectives, per_device(): lax.psum((inner(basis, basis, total), inner(basis, snapshots, total), inn...  42.8 us
    another operation x24, other arithmetic, orthonormal(): factor = jnp.linalg.cholesky(jnp.dot(block.T, block, precision=HIGH))  28.8 us
    another operation x16, other arithmetic, orthonormal(): block = jax.scipy.linalg.solve_triangular(factor, block.T, lower=True).T  24.8 us
    dot_general x3, matrix products, inner(): lax.dot_general(left, right, (((1,), (1,)), ((), ())), precision=HIGH, pr...  6.85 us
    another operation x3, other arithmetic, per_device(): lower = jnp.linalg.cholesky(snap_gram - cross - cross.T + bent)  6.52 us
    another operation x2, other arithmetic, per_device(): fresh = jax.scipy.linalg.solve_triangular(lower, residual, lower=True)  5.55 us
    dot_general x2, matrix products, remove(): return block - jnp.dot(coeffs.T, basis, precision=HIGH)  3.74 us

commit v1 on v0

v1 whole, which is shorter than its diff:
```python
import functools

import jax
import jax.numpy as jnp
from jax import lax
from jax.experimental import pallas as pl
from jax.experimental.pallas import tpu as pltpu
from jax.sharding import PartitionSpec as P

ITERS = 4
AXES = ("gx", "gy", "gz")
HIGH = lax.Precision.HIGHEST
NN = (((1,), (0,)), ((), ()))
NT = (((1,), (1,)), ((), ()))


def dot(a, b, dims=NN):
    return lax.dot_general(a, b, dims, precision=HIGH, preferred_element_type=jnp.float32)


def split(x):
    high = x.astype(jnp.bfloat16)
    return high, (x - high.astype(jnp.float32)).astype(jnp.bfloat16)


def blocks_of(columns, most):
    width = columns
    while width > most and width % 256 == 0:
        width //= 2
    return width


def gram_kernel(scale, steps, snap_ref, basis_ref, out_ref, acc_ref):
    step = pl.program_id(0)
    snap_high, snap_low = split(snap_ref[...])
    basis_high, basis_low = split(basis_ref[...])
    both = jnp.concatenate([snap_high, basis_high, snap_low, basis_low], axis=0)
    product = lax.dot_general(both, both, NT, preferred_element_type=jnp.float32)

    @pl.when(step == 0)
    def _():
        acc_ref[...] = product

    @pl.when(step > 0)
    def _():
        acc_ref[...] += product

    @pl.when(step == steps - 1)
    def _():
        count = out_ref.shape[0]
        total = acc_ref[...]
        rows = total[:count] + total[count:]
        out_ref[...] = (rows[:, :count] + rows[:, count:]) * scale


def gram(snapshots, basis, total):
    new, columns = snapshots.shape
    modes = basis.shape[0]
    width = blocks_of(columns, 2048)
    steps = columns // width
    count = new + modes
    return pl.pallas_call(
        functools.partial(gram_kernel, 1.0 / total, steps),
        out_shape=jax.ShapeDtypeStruct((count, count), jnp.float32),
        grid=(steps,),
        in_specs=[
            pl.BlockSpec((new, width), lambda i: (0, i)),
            pl.BlockSpec((modes, width), lambda i: (0, i)),
        ],
        out_specs=pl.BlockSpec((count, count), lambda i: (0, 0)),
        scratch_shapes=[pltpu.VMEM((2 * count, 2 * count), jnp.float32)],
        compiler_params=pltpu.CompilerParams(dimension_semantics=("arbitrary",)),
        name="gram",
    )(snapshots, basis)


def all_sum(x, sizes):
    for axis, size in sizes:
        if size & (size - 1):
            x = lax.psum(x, axis)
            continue
        bit = 1
        while bit < size:
            x = x + lax.ppermute(x, axis, [(i, i ^ bit) for i in range(size)])
            bit *= 2
    return x


def normalize(square, parts):
    n = square.shape[0]
    row = lax.broadcasted_iota(jnp.int32, (n, 1), 0)
    for j in range(n - 1):
        inverse = 1.0 / square[j : j + 1, j : j + 1]
        column = jnp.where(row > j, square[:, j : j + 1], 0.0)
        parts = [p - column * (p[j : j + 1] * inverse) for p in parts]
        square = square - column * (square[j : j + 1] * inverse)
    diagonal = lax.broadcasted_iota(jnp.int32, (n, n), 0) == lax.broadcasted_iota(jnp.int32, (n, n), 1)
    pivots = jnp.sum(jnp.where(diagonal, square, 0.0), axis=1, keepdims=True)
    scale = lax.rsqrt(pivots)
    return [p * scale for p in parts]


def update_kernel(
    width, sums_ref, sigma_ref, snap_ref, basis_ref, modes_ref, values_ref, data_ref, out_ref, step_ref, in_sem, out_sem
):
    modes = basis_ref.shape[0]
    new, columns = snap_ref.shape
    count = new + modes
    loads = [
        pltpu.make_async_copy(snap_ref, data_ref.at[pl.ds(0, new)], in_sem.at[0]),
        pltpu.make_async_copy(basis_ref, data_ref.at[pl.ds(new, modes)], in_sem.at[1]),
    ]
    for load in loads:
        load.start()

    gram_all = sums_ref[...]
    snap_gram = gram_all[:new, :new]
    first_t = gram_all[:new, new:]
    first = gram_all[new:, :new]
    corr = gram_all[new:, new:]
    joined = 2.0 * first - dot(corr, first)
    joined_t = 2.0 * first_t - dot(first_t, corr)
    rest = first_t - dot(joined_t, corr)
    residual = snap_gram - dot(joined_t, first) - dot(rest, joined)
    eye = (
        lax.broadcasted_iota(jnp.int32, (modes, modes), 0) == lax.broadcasted_iota(jnp.int32, (modes, modes), 1)
    )
    sigma_row = sigma_ref[...]
    sigma2 = sigma_row * sigma_row
    corner = jnp.where(eye, sigma2, 0.0) + dot(joined, joined_t)
    bend = dot(joined, residual)
    eye_new = (
        lax.broadcasted_iota(jnp.int32, (new, new), 0) == lax.broadcasted_iota(jnp.int32, (new, new), 1)
    ).astype(jnp.float32)

    half = step_ref.shape[1] // 2
    step_ref[...] = jnp.zeros_like(step_ref)
    step_ref[:modes, :modes] = corner
    step_ref[:modes, modes:count] = joined
    step_ref[:modes, half : half + modes] = corner
    step_ref[:modes, half + modes : half + count] = bend
    step_ref[modes:, :modes] = joined_t
    step_ref[modes:, modes:count] = eye_new
    step_ref[modes:, half : half + modes] = joined_t
    step_ref[modes:, half + modes : half + count] = residual

    left = step_ref[:modes, :half]
    right = step_ref[:modes, half:]
    for step in range(ITERS):
        if step:
            both = dot(right[:, :count], step_ref[...])
            left, right = both[:, :half], both[:, half:]
        for repeat in range(2):
            square = dot(left, right, NT)
            left, right = normalize(square, [left, right])

    after = dot(right[:, :count], step_ref[:, :half])
    lane = lax.broadcasted_iota(jnp.int32, (modes, half), 1)
    spread = jnp.concatenate([sigma_row, jnp.zeros((1, half - modes), jnp.float32)], axis=1)
    part = jnp.where(lane < modes, left * spread, jnp.where(lane < count, after, 0.0))
    ritz = dot(jnp.ones((8, half), jnp.float32), part * part, NT)
    values_ref[...] = jnp.sqrt(ritz[:1])

    y = left[:, :modes]
    z = left[:, modes:count]
    weights = jnp.concatenate([z, y - dot(z, joined_t)], axis=1)
    high, low = split(weights)
    left_side = jnp.concatenate(
        [jnp.concatenate([high, high], axis=1), jnp.concatenate([low, low], axis=1)], axis=0
    )
    for load in loads:
        load.wait()
    stores = []
    for i in range(columns // width):
        piece = pl.ds(i * width, width)
        data_high, data_low = split(data_ref[:, piece])
        data = jnp.concatenate([data_high, data_low], axis=0)
        product = lax.dot_general(left_side, data, NN, preferred_element_type=jnp.float32)
        out_ref[:, piece] = product[:modes] + product[modes:]
        store = pltpu.make_async_copy(out_ref.at[:, piece], modes_ref.at[:, piece], out_sem.at[i])
        store.start()
        stores.append(store)
    for store in stores:
        store.wait()


def update(sums, sigma, snapshots, basis):
    new, columns = snapshots.shape
    modes = basis.shape[0]
    count = new + modes
    width = blocks_of(columns, 2048)
    half = -(-count // 128) * 128
    return pl.pallas_call(
        functools.partial(update_kernel, width),
        out_shape=(
            jax.ShapeDtypeStruct((modes, columns), jnp.float32),
            jax.ShapeDtypeStruct((1, modes), jnp.float32),
        ),
        in_specs=[
            pl.BlockSpec(memory_space=pltpu.VMEM),
            pl.BlockSpec(memory_space=pltpu.VMEM),
            pl.BlockSpec(memory_space=pl.ANY),
            pl.BlockSpec(memory_space=pl.ANY),
        ],
        out_specs=(pl.BlockSpec(memory_space=pl.ANY), pl.BlockSpec(memory_space=pltpu.VMEM)),
        scratch_shapes=[
            pltpu.VMEM((count, columns), jnp.float32),
            pltpu.VMEM((modes, columns), jnp.float32),
            pltpu.VMEM((count, 2 * half), jnp.float32),
            pltpu.SemaphoreType.DMA((2,)),
            pltpu.SemaphoreType.DMA((columns // width,)),
        ],
        name="update",
    )(sums, sigma, snapshots, basis)


def per_device(sizes, basis, sigma, snapshots):
    total = basis.shape[1] * 1.0
    for _, size in sizes:
        total *= size
    sums = all_sum(gram(snapshots, basis, total), sizes)
    modes, values = update(sums, sigma.reshape(1, -1), snapshots, basis)
    return modes, values.reshape(-1)


def solution(mesh):
    placed = (P(None, AXES), P(), P(None, AXES))
    sizes = tuple((axis, mesh.shape[axis]) for axis in AXES)
    return jax.shard_map(
        functools.partial(per_device, sizes),
        mesh=mesh,
        in_specs=placed,
        out_specs=(P(None, AXES), P()),
        check_vma=False,
    )
```

time: 133 us -> 53.9 us (0.41)
  other arithmetic: 65.9 us -> 1.45 us
  blocking collectives: 42.8 us -> 0 us
  Pallas kernels: 0 us -> 31.2 us
  matrix products: 20.8 us -> 0 us
  starting transfers between devices: 0 us -> 11 us
  waiting for transfers between devices: 0 us -> 9.37 us
  local copies, waits for them, and re-layouts: 1.98 us -> 0 us
    another operation x45 -> x0, other arithmetic: 65.7 us -> none  [the longest x24 28.8 us: orthonormal(): factor = jnp.linalg.cholesky(jnp.dot(block.T, block, precision=HIGH))]
    psum x1 -> x0, blocking collectives: 42.8 us -> none  [per_device(): lax.psum((inner(basis, basis, total), inner(basis, snapshots, total), inn...]
    pallas_call x0 -> x2, Pallas kernels: none -> 31.2 us  [the longest x1 26.9 us: update(): pl.pallas_call(functools.partial(update_kernel, width), out_shape=(jax.Sh...]
    dot_general x25 -> x0, matrix products: 17.1 us -> none  [the longest x3 6.85 us: inner(): lax.dot_general(left, right, (((1,), (1,)), ((), ())), precision=HIGH, pr...]
    ppermute x0 -> x5, starting transfers between devices: none -> 11 us  [all_sum(): x = x + lax.ppermute(x, axis, [(i, i ^ bit) for i in range(size)])]
    ppermute x0 -> x5, waiting for transfers between devices: none -> 9.37 us  [all_sum(): x = x + lax.ppermute(x, axis, [(i, i ^ bit) for i in range(size)])]
    another operation x9 -> x0, matrix products: 3.77 us -> none  [the longest x1 1.91 us: per_device(): fresh = jax.scipy.linalg.solve_triangular(lower, residual, lower=True)]
    add x0 -> x5, other arithmetic: none -> 1.45 us  [all_sum(): x = x + lax.ppermute(x, axis, [(i, i ^ bit) for i in range(size)])]
  transfers between devices with their start and end apart: 0 -> 5, of which waited for: 0 -> 5; matrix products, arithmetic and copies ran while one was open for 0% -> 0% of each run, Pallas kernels for 0% -> 0%
where the time goes in v1:
time: 53.9 us; the launch traced here: 53.6 us
  Pallas kernels  31.2 us (58%)
  starting transfers between devices  11 us (20%)
  waiting for transfers between devices  9.37 us (17%)
  other arithmetic  1.45 us (3%)
  between operations  0.64 us (1%)
    pallas_call x1, Pallas kernels, update(): pl.pallas_call(functools.partial(update_kernel, width), out_shape=(jax.Sh...  26.9 us
    ppermute x5, starting transfers between devices, all_sum(): x = x + lax.ppermute(x, axis, [(i, i ^ bit) for i in range(size)])  11 us
    ppermute x5, waiting for transfers between devices, all_sum(): x = x + lax.ppermute(x, axis, [(i, i ^ bit) for i in range(size)])  9.37 us
    pallas_call x1, Pallas kernels, gram(): pl.pallas_call(functools.partial(gram_kernel, 1.0 / total, steps), out_sh...  4.26 us
    add x5, other arithmetic, all_sum(): x = x + lax.ppermute(x, axis, [(i, i ^ bit) for i in range(size)])  1.45 us
  transfers between devices with their start and end apart: 5, of which 5 were waited for; matrix products, arithmetic and copies ran while one was open for 0% of the time, Pallas kernels for 0%

profile of v1, /device:TPU:0, one launch (start us, length us, event | category | flops | bytes accessed | tf_op | source)
XLA Modules:
  0.0 53.6 jit_solution(16330998436901786097)
XLA Ops:
  0.6 4.3 %gram.1 = f32[96,96]{1,0:T(8,128)} custom-call(f32[64,8192]{1,0:T(8,128)} %snap_ref.3, f32[32,8192]{1,0:T(8,128)} %basis_ref.3), custom_call_target="tpu_custom_call" | custom-call | tf_op jit(solution)/shard_map/gram/pallas_call | solution.py:62
  4.9 0.5 collective-permute-start
  5.4 1.1 %collective-permute-done = f32[96,96]{1,0:T(8,128)S(1)} collective-permute-done((f32[96,96]{1,0:T(8,128)}, f32[96,96]{1,0:T(8,128)S(1)}, u32[]{:S(2)}, u32[]{:S(2)}) %collective-permute-start) | collective-permute-done | bytes 36896 | tf_op jit(solution)/shard_map/ppermute | solution.py:84
  6.5 0.8 %add.15 = f32[96,96]{1,0:T(8,128)S(1)} add(f32[96,96]{1,0:T(8,128)} %gram.1, f32[96,96]{1,0:T(8,128)S(1)} %collective-permute-done) | non-fusion elementwise | flops 9216 | bytes 110592 | tf_op jit(solution)/shard_map/add | solution.py:84
  7.3 2.8 %collective-permute-start.1 = (f32[96,96]{1,0:T(8,128)S(1)}, f32[96,96]{1,0:T(8,128)S(1)}, u32[]{:S(2)}, u32[]{:S(2)}) collective-permute-start(f32[96,96]{1,0:T(8,128)S(1)} %add.15), channel_id=1, source_target_pairs={{0,4},{4,0},{8,12},{12,8},{1,5},{5,1},{9,13},{13,9},{2,6},{6,2},{1... | collective-permute-start | bytes 110600 | tf_op jit(solution)/shard_map/ppermute | solution.py:84
  10.1 2.1 %collective-permute-done.1 = f32[96,96]{1,0:T(8,128)S(1)} collective-permute-done((f32[96,96]{1,0:T(8,128)S(1)}, f32[96,96]{1,0:T(8,128)S(1)}, u32[]{:S(2)}, u32[]{:S(2)}) %collective-permute-start.1) | collective-permute-done | bytes 36896 | tf_op jit(solution)/shard_map/ppermute | solution.py:84
  12.2 2.1 %collective-permute-start.2 = (f32[96,96]{1,0:T(8,128)S(1)}, f32[96,96]{1,0:T(8,128)S(1)}, u32[]{:S(2)}, u32[]{:S(2)}) collective-permute-start(f32[96,96]{1,0:T(8,128)S(1)} %add.16), channel_id=1, source_target_pairs={{0,8},{4,12},{8,0},{12,4},{1,9},{5,13},{9,1},{13,5},{2,10},{6,14},... | collective-permute-start | bytes 110600 | tf_op jit(solution)/shard_map/ppermute | solution.py:84
  14.3 2.1 %collective-permute-done.2 = f32[96,96]{1,0:T(8,128)S(1)} collective-permute-done((f32[96,96]{1,0:T(8,128)S(1)}, f32[96,96]{1,0:T(8,128)S(1)}, u32[]{:S(2)}, u32[]{:S(2)}) %collective-permute-start.2) | collective-permute-done | bytes 36896 | tf_op jit(solution)/shard_map/ppermute | solution.py:84
  16.4 2.1 %collective-permute-start.3 = (f32[96,96]{1,0:T(8,128)S(1)}, f32[96,96]{1,0:T(8,128)S(1)}, u32[]{:S(2)}, u32[]{:S(2)}) collective-permute-start(f32[96,96]{1,0:T(8,128)S(1)} %add.17), channel_id=1, source_target_pairs={{0,1},{1,0},{2,3},{3,2},{4,5},{5,4},{6,7},{7,6},{8,9},{9,8},{10,11... | collective-permute-start | bytes 110600 | tf_op jit(solution)/shard_map/ppermute | solution.py:84
  18.5 2.1 %collective-permute-done.3 = f32[96,96]{1,0:T(8,128)S(1)} collective-permute-done((f32[96,96]{1,0:T(8,128)S(1)}, f32[96,96]{1,0:T(8,128)S(1)}, u32[]{:S(2)}, u32[]{:S(2)}) %collective-permute-start.3) | collective-permute-done | bytes 36896 | tf_op jit(solution)/shard_map/ppermute | solution.py:84
  20.6 3.4 %collective-permute-start.4 = (f32[96,96]{1,0:T(8,128)S(1)}, f32[96,96]{1,0:T(8,128)S(1)}, u32[]{:S(2)}, u32[]{:S(2)}) collective-permute-start(f32[96,96]{1,0:T(8,128)S(1)} %add.18), channel_id=1, source_target_pairs={{0,2},{1,3},{2,0},{3,1},{4,6},{5,7},{6,4},{7,5},{8,10},{9,11},{10,... | collective-permute-start | bytes 110600 | tf_op jit(solution)/shard_map/ppermute | solution.py:84
  24.0 2.1 %collective-permute-done.4 = f32[96,96]{1,0:T(8,128)S(1)} collective-permute-done((f32[96,96]{1,0:T(8,128)S(1)}, f32[96,96]{1,0:T(8,128)S(1)}, u32[]{:S(2)}, u32[]{:S(2)}) %collective-permute-start.4) | collective-permute-done | bytes 36896 | tf_op jit(solution)/shard_map/ppermute | solution.py:84
  26.1 0.6 %add.19.sums_ref = f32[96,96]{1,0:T(8,128)} add(f32[96,96]{1,0:T(8,128)S(1)} %add.18, f32[96,96]{1,0:T(8,128)S(1)} %collective-permute-done.4) | non-fusion elementwise | flops 9216 | bytes 110592 | tf_op jit(solution)/shard_map/add | solution.py:84
  26.7 26.9 %update.1 = (f32[32,8192]{1,0:T(8,128)}, f32[1,32]{1,0:T(1,128)}) custom-call(f32[96,96]{1,0:T(8,128)} %add.19.sums_ref, f32[1,32]{1,0:T(1,128)} %bitcast.2, f32[64,8192]{1,0:T(8,128)} %snap_ref.3, f32[32,8192]{1,0:T(8,128)} %basis_ref.3), custom_call_target="tpu_custom_call" | custom-call | tf_op jit(solution)/shard_map/update/pallas_call | solution.py:193
  (3 shorter events, 0.0 us)
Async XLA Ops:
  4.9 1.6 %collective-permute-start = (f32[96,96]{1,0:T(8,128)}, f32[96,96]{1,0:T(8,128)S(1)}, u32[]{:S(2)}, u32[]{:S(2)}) collective-permute-start(f32[96,96]{1,0:T(8,128)} %gram.1), channel_id=1, source_target_pairs={{0,16},{16,0},{1,17},{17,1},{2,18},{18,2},{3,19},{19,3},{4,20},{20... | collective-permute-start | bytes 110600 | tf_op jit(solution)/shard_map/ppermute | solution.py:84
  7.3 4.9 %collective-permute-start.1 = (f32[96,96]{1,0:T(8,128)S(1)}, f32[96,96]{1,0:T(8,128)S(1)}, u32[]{:S(2)}, u32[]{:S(2)}) collective-permute-start(f32[96,96]{1,0:T(8,128)S(1)} %add.15), channel_id=1, source_target_pairs={{0,4},{4,0},{8,12},{12,8},{1,5},{5,1},{9,13},{13,9},{2,6},{6,2},{1... | collective-permute-start | bytes 110600 | tf_op jit(solution)/shard_map/ppermute | solution.py:84
  12.2 4.2 %collective-permute-start.2 = (f32[96,96]{1,0:T(8,128)S(1)}, f32[96,96]{1,0:T(8,128)S(1)}, u32[]{:S(2)}, u32[]{:S(2)}) collective-permute-start(f32[96,96]{1,0:T(8,128)S(1)} %add.16), channel_id=1, source_target_pairs={{0,8},{4,12},{8,0},{12,4},{1,9},{5,13},{9,1},{13,5},{2,10},{6,14},... | collective-permute-start | bytes 110600 | tf_op jit(solution)/shard_map/ppermute | solution.py:84
  16.4 4.2 %collective-permute-start.3 = (f32[96,96]{1,0:T(8,128)S(1)}, f32[96,96]{1,0:T(8,128)S(1)}, u32[]{:S(2)}, u32[]{:S(2)}) collective-permute-start(f32[96,96]{1,0:T(8,128)S(1)} %add.17), channel_id=1, source_target_pairs={{0,1},{1,0},{2,3},{3,2},{4,5},{5,4},{6,7},{7,6},{8,9},{9,8},{10,11... | collective-permute-start | bytes 110600 | tf_op jit(solution)/shard_map/ppermute | solution.py:84
  20.6 5.5 %collective-permute-start.4 = (f32[96,96]{1,0:T(8,128)S(1)}, f32[96,96]{1,0:T(8,128)S(1)}, u32[]{:S(2)}, u32[]{:S(2)}) collective-permute-start(f32[96,96]{1,0:T(8,128)S(1)} %add.18), channel_id=1, source_target_pairs={{0,2},{1,3},{2,0},{3,1},{4,6},{5,7},{6,4},{7,5},{8,10},{9,11},{10,... | collective-permute-start | bytes 110600 | tf_op jit(solution)/shard_map/ppermute | solution.py:84

commit v2 on v1

--- a/solution.py
+++ b/solution.py
@@ -87,17 +87,40 @@
 
 
 def normalize(square, parts):
-    n = square.shape[0]
-    row = lax.broadcasted_iota(jnp.int32, (n, 1), 0)
-    for j in range(n - 1):
-        inverse = 1.0 / square[j : j + 1, j : j + 1]
-        column = jnp.where(row > j, square[:, j : j + 1], 0.0)
-        parts = [p - column * (p[j : j + 1] * inverse) for p in parts]
-        square = square - column * (square[j : j + 1] * inverse)
-    diagonal = lax.broadcasted_iota(jnp.int32, (n, n), 0) == lax.broadcasted_iota(jnp.int32, (n, n), 1)
-    pivots = jnp.sum(jnp.where(diagonal, square, 0.0), axis=1, keepdims=True)
-    scale = lax.rsqrt(pivots)
-    return [p * scale for p in parts]
+    n, lanes = square.shape[0], parts[0].shape[1]
+    groups = n // 8
+    row = lax.broadcasted_iota(jnp.int32, (8, lanes), 0)
+    parts = [[p[8 * q : 8 * q + 8] for q in range(groups)] for p in parts]
+    spread = [
+        [
+            jnp.broadcast_to(square[8 * q : 8 * q + 8, l : l + 1], (8, lanes)) if q >= l // 8 else None
+            for q in range(groups)
+        ]
+        for l in range(n)
+    ]
+    pivots = [jnp.ones((8, lanes), jnp.float32) for _ in range(groups)]
+    for k in range(n):
+        own, r = k // 8, k % 8
+        column = spread[k]
+        pivot = jnp.broadcast_to(column[own][r : r + 1], (8, lanes))
+        pivots[own] = jnp.where(row == r, pivot, pivots[own])
+        inverse = 1.0 / pivot
+        for l in range(k + 1, n):
+            entry = jnp.broadcast_to(column[l // 8][l % 8 : l % 8 + 1], (8, lanes))
+            for q in range(l // 8, groups):
+                if l == k + 1:
+                    spread[l][q] = spread[l][q] - (column[q] * entry) * inverse
+                else:
+                    spread[l][q] = spread[l][q] - column[q] * (entry * inverse)
+        for p in parts:
+            line = jnp.broadcast_to(p[own][r : r + 1], (8, lanes)) * inverse
+            for q in range(own, groups):
+                if q > own:
+                    p[q] = p[q] - column[q] * line
+                elif r < 7:
+                    p[q] = p[q] - jnp.where(row > r, column[q], 0.0) * line
+    scales = [lax.rsqrt(p) for p in pivots]
+    return [jnp.concatenate([x * s for x, s in zip(p, scales)], axis=0) for p in parts]
 
 
 def update_kernel(

time: 53.9 us -> 39.3 us (0.73)
  Pallas kernels: 31.2 us -> 16.6 us
    pallas_call x1, Pallas kernels: 26.9 us -> 12.3 us  [update(): pl.pallas_call(functools.partial(update_kernel, width), out_shape=(jax.Sh...]
where the time goes in v2:
time: 39.3 us; the launch traced here: 39 us
  Pallas kernels  16.6 us (42%)
  starting transfers between devices  11 us (28%)
  waiting for transfers between devices  9.37 us (24%)
  other arithmetic  1.45 us (4%)
  between operations  0.64 us (2%)
    pallas_call x1, Pallas kernels, update(): pl.pallas_call(functools.partial(update_kernel, width), out_shape=(jax.Sh...  12.3 us
    ppermute x5, starting transfers between devices, all_sum(): x = x + lax.ppermute(x, axis, [(i, i ^ bit) for i in range(size)])  11 us
    ppermute x5, waiting for transfers between devices, all_sum(): x = x + lax.ppermute(x, axis, [(i, i ^ bit) for i in range(size)])  9.37 us
    pallas_call x1, Pallas kernels, gram(): pl.pallas_call(functools.partial(gram_kernel, 1.0 / total, steps), out_sh...  4.26 us
    add x5, other arithmetic, all_sum(): x = x + lax.ppermute(x, axis, [(i, i ^ bit) for i in range(size)])  1.45 us
  transfers between devices with their start and end apart: 5, of which 5 were waited for; matrix products, arithmetic and copies ran while one was open for 0% of the time, Pallas kernels for 0%

profile of v2, /device:TPU:0, one launch (start us, length us, event | category | flops | bytes accessed | tf_op | source)
XLA Modules:
  0.0 39.0 jit_solution(13431687130288539887)
XLA Ops:
  0.6 4.3 %gram.1 = f32[96,96]{1,0:T(8,128)} custom-call(f32[64,8192]{1,0:T(8,128)} %snap_ref.3, f32[32,8192]{1,0:T(8,128)} %basis_ref.3), custom_call_target="tpu_custom_call" | custom-call | tf_op jit(solution)/shard_map/gram/pallas_call | solution.py:62
  4.9 0.5 %collective-permute-start = (f32[96,96]{1,0:T(8,128)}, f32[96,96]{1,0:T(8,128)S(1)}, u32[]{:S(2)}, u32[]{:S(2)}) collective-permute-start(f32[96,96]{1,0:T(8,128)} %gram.1), channel_id=1, source_target_pairs={{0,16},{16,0},{1,17},{17,1},{2,18},{18,2},{3,19},{19,3},{4,20},{20... | collective-permute-start | bytes 110600 | tf_op jit(solution)/shard_map/ppermute | solution.py:84
  5.4 1.1 %collective-permute-done = f32[96,96]{1,0:T(8,128)S(1)} collective-permute-done((f32[96,96]{1,0:T(8,128)}, f32[96,96]{1,0:T(8,128)S(1)}, u32[]{:S(2)}, u32[]{:S(2)}) %collective-permute-start) | collective-permute-done | bytes 36896 | tf_op jit(solution)/shard_map/ppermute | solution.py:84
  6.5 0.8 %add.15 = f32[96,96]{1,0:T(8,128)S(1)} add(f32[96,96]{1,0:T(8,128)} %gram.1, f32[96,96]{1,0:T(8,128)S(1)} %collective-permute-done) | non-fusion elementwise | flops 9216 | bytes 110592 | tf_op jit(solution)/shard_map/add | solution.py:84
  7.3 2.8 %collective-permute-start.1 = (f32[96,96]{1,0:T(8,128)S(1)}, f32[96,96]{1,0:T(8,128)S(1)}, u32[]{:S(2)}, u32[]{:S(2)}) collective-permute-start(f32[96,96]{1,0:T(8,128)S(1)} %add.15), channel_id=1, source_target_pairs={{0,4},{4,0},{8,12},{12,8},{1,5},{5,1},{9,13},{13,9},{2,6},{6,2},{1... | collective-permute-start | bytes 110600 | tf_op jit(solution)/shard_map/ppermute | solution.py:84
  10.1 2.1 %collective-permute-done.1 = f32[96,96]{1,0:T(8,128)S(1)} collective-permute-done((f32[96,96]{1,0:T(8,128)S(1)}, f32[96,96]{1,0:T(8,128)S(1)}, u32[]{:S(2)}, u32[]{:S(2)}) %collective-permute-start.1) | collective-permute-done | bytes 36896 | tf_op jit(solution)/shard_map/ppermute | solution.py:84
  12.2 2.1 %collective-permute-start.2 = (f32[96,96]{1,0:T(8,128)S(1)}, f32[96,96]{1,0:T(8,128)S(1)}, u32[]{:S(2)}, u32[]{:S(2)}) collective-permute-start(f32[96,96]{1,0:T(8,128)S(1)} %add.16), channel_id=1, source_target_pairs={{0,8},{4,12},{8,0},{12,4},{1,9},{5,13},{9,1},{13,5},{2,10},{6,14},... | collective-permute-start | bytes 110600 | tf_op jit(solution)/shard_map/ppermute | solution.py:84
  14.3 2.1 %collective-permute-done.2 = f32[96,96]{1,0:T(8,128)S(1)} collective-permute-done((f32[96,96]{1,0:T(8,128)S(1)}, f32[96,96]{1,0:T(8,128)S(1)}, u32[]{:S(2)}, u32[]{:S(2)}) %collective-permute-start.2) | collective-permute-done | bytes 36896 | tf_op jit(solution)/shard_map/ppermute | solution.py:84
  16.4 2.1 %collective-permute-start.3 = (f32[96,96]{1,0:T(8,128)S(1)}, f32[96,96]{1,0:T(8,128)S(1)}, u32[]{:S(2)}, u32[]{:S(2)}) collective-permute-start(f32[96,96]{1,0:T(8,128)S(1)} %add.17), channel_id=1, source_target_pairs={{0,1},{1,0},{2,3},{3,2},{4,5},{5,4},{6,7},{7,6},{8,9},{9,8},{10,11... | collective-permute-start | bytes 110600 | tf_op jit(solution)/shard_map/ppermute | solution.py:84
  18.5 2.1 %collective-permute-done.3 = f32[96,96]{1,0:T(8,128)S(1)} collective-permute-done((f32[96,96]{1,0:T(8,128)S(1)}, f32[96,96]{1,0:T(8,128)S(1)}, u32[]{:S(2)}, u32[]{:S(2)}) %collective-permute-start.3) | collective-permute-done | bytes 36896 | tf_op jit(solution)/shard_map/ppermute | solution.py:84
  20.6 3.4 %collective-permute-start.4 = (f32[96,96]{1,0:T(8,128)S(1)}, f32[96,96]{1,0:T(8,128)S(1)}, u32[]{:S(2)}, u32[]{:S(2)}) collective-permute-start(f32[96,96]{1,0:T(8,128)S(1)} %add.18), channel_id=1, source_target_pairs={{0,2},{1,3},{2,0},{3,1},{4,6},{5,7},{6,4},{7,5},{8,10},{9,11},{10,... | collective-permute-start | bytes 110600 | tf_op jit(solution)/shard_map/ppermute | solution.py:84
  24.0 2.1 %collective-permute-done.4 = f32[96,96]{1,0:T(8,128)S(1)} collective-permute-done((f32[96,96]{1,0:T(8,128)S(1)}, f32[96,96]{1,0:T(8,128)S(1)}, u32[]{:S(2)}, u32[]{:S(2)}) %collective-permute-start.4) | collective-permute-done | bytes 36896 | tf_op jit(solution)/shard_map/ppermute | solution.py:84
  26.1 0.6 %add.19.sums_ref = f32[96,96]{1,0:T(8,128)} add(f32[96,96]{1,0:T(8,128)S(1)} %add.18, f32[96,96]{1,0:T(8,128)S(1)} %collective-permute-done.4) | non-fusion elementwise | flops 9216 | bytes 110592 | tf_op jit(solution)/shard_map/add | solution.py:84
  26.7 12.3 %update.1 = (f32[32,8192]{1,0:T(8,128)}, f32[1,32]{1,0:T(1,128)}) custom-call(f32[96,96]{1,0:T(8,128)} %add.19.sums_ref, f32[1,32]{1,0:T(1,128)} %bitcast.2, f32[64,8192]{1,0:T(8,128)} %snap_ref.3, f32[32,8192]{1,0:T(8,128)} %basis_ref.3), custom_call_target="tpu_custom_call" | custom-call | tf_op jit(solution)/shard_map/update/pallas_call | solution.py:216
  (3 shorter events, 0.0 us)
Async XLA Ops:
  4.9 1.6 %collective-permute-start = (f32[96,96]{1,0:T(8,128)}, f32[96,96]{1,0:T(8,128)S(1)}, u32[]{:S(2)}, u32[]{:S(2)}) collective-permute-start(f32[96,96]{1,0:T(8,128)} %gram.1), channel_id=1, source_target_pairs={{0,16},{16,0},{1,17},{17,1},{2,18},{18,2},{3,19},{19,3},{4,20},{20... | collective-permute-start | bytes 110600 | tf_op jit(solution)/shard_map/ppermute | solution.py:84
  7.3 4.9 %collective-permute-start.1 = (f32[96,96]{1,0:T(8,128)S(1)}, f32[96,96]{1,0:T(8,128)S(1)}, u32[]{:S(2)}, u32[]{:S(2)}) collective-permute-start(f32[96,96]{1,0:T(8,128)S(1)} %add.15), channel_id=1, source_target_pairs={{0,4},{4,0},{8,12},{12,8},{1,5},{5,1},{9,13},{13,9},{2,6},{6,2},{1... | collective-permute-start | bytes 110600 | tf_op jit(solution)/shard_map/ppermute | solution.py:84
  12.2 4.2 %collective-permute-start.2 = (f32[96,96]{1,0:T(8,128)S(1)}, f32[96,96]{1,0:T(8,128)S(1)}, u32[]{:S(2)}, u32[]{:S(2)}) collective-permute-start(f32[96,96]{1,0:T(8,128)S(1)} %add.16), channel_id=1, source_target_pairs={{0,8},{4,12},{8,0},{12,4},{1,9},{5,13},{9,1},{13,5},{2,10},{6,14},... | collective-permute-start | bytes 110600 | tf_op jit(solution)/shard_map/ppermute | solution.py:84
  16.4 4.2 %collective-permute-start.3 = (f32[96,96]{1,0:T(8,128)S(1)}, f32[96,96]{1,0:T(8,128)S(1)}, u32[]{:S(2)}, u32[]{:S(2)}) collective-permute-start(f32[96,96]{1,0:T(8,128)S(1)} %add.17), channel_id=1, source_target_pairs={{0,1},{1,0},{2,3},{3,2},{4,5},{5,4},{6,7},{7,6},{8,9},{9,8},{10,11... | collective-permute-start | bytes 110600 | tf_op jit(solution)/shard_map/ppermute | solution.py:84
  20.6 5.5 %collective-permute-start.4 = (f32[96,96]{1,0:T(8,128)S(1)}, f32[96,96]{1,0:T(8,128)S(1)}, u32[]{:S(2)}, u32[]{:S(2)}) collective-permute-start(f32[96,96]{1,0:T(8,128)S(1)} %add.18), channel_id=1, source_target_pairs={{0,2},{1,3},{2,0},{3,1},{4,6},{5,7},{6,4},{7,5},{8,10},{9,11},{10,... | collective-permute-start | bytes 110600 | tf_op jit(solution)/shard_map/ppermute | solution.py:84

commit v3 on v2

--- a/solution.py
+++ b/solution.py
@@ -8,6 +8,8 @@
 from jax.sharding import PartitionSpec as P
 
 ITERS = 4
+GRAM_WIDTH = 4096
+GRANT = 24 * 1024 * 1024
 AXES = ("gx", "gy", "gz")
 HIGH = lax.Precision.HIGHEST
 NN = (((1,), (0,)), ((), ()))
@@ -30,46 +32,47 @@
     return width
 
 
-def gram_kernel(scale, steps, snap_ref, basis_ref, out_ref, acc_ref):
-    step = pl.program_id(0)
-    snap_high, snap_low = split(snap_ref[...])
-    basis_high, basis_low = split(basis_ref[...])
-    both = jnp.concatenate([snap_high, basis_high, snap_low, basis_low], axis=0)
-    product = lax.dot_general(both, both, NT, preferred_element_type=jnp.float32)
-
-    @pl.when(step == 0)
-    def _():
-        acc_ref[...] = product
-
-    @pl.when(step > 0)
-    def _():
-        acc_ref[...] += product
-
-    @pl.when(step == steps - 1)
-    def _():
-        count = out_ref.shape[0]
-        total = acc_ref[...]
-        rows = total[:count] + total[count:]
-        out_ref[...] = (rows[:, :count] + rows[:, count:]) * scale
+def gram_kernel(scale, width, snap_ref, basis_ref, out_ref, data_ref, sem):
+    new, columns = snap_ref.shape
+    modes = basis_ref.shape[0]
+    count = new + modes
+    steps = columns // width
+    loads = []
+    for i in range(steps):
+        piece = pl.ds(i * width, width)
+        pair = [
+            pltpu.make_async_copy(snap_ref.at[:, piece], data_ref.at[pl.ds(0, new), piece], sem.at[0, i]),
+            pltpu.make_async_copy(basis_ref.at[:, piece], data_ref.at[pl.ds(new, modes), piece], sem.at[1, i]),
+        ]
+        for load in pair:
+            load.start()
+        loads.append(pair)
+    total = None
+    for i in range(steps):
+        for load in loads[i]:
+            load.wait()
+        both = jnp.concatenate(split(data_ref[:, pl.ds(i * width, width)]), axis=0)
+        product = lax.dot_general(both, both, NT, preferred_element_type=jnp.float32)
+        total = product if total is None else total + product
+    rows = total[:count] + total[count:]
+    out_ref[...] = (rows[:, :count] + rows[:, count:]) * scale
 
 
 def gram(snapshots, basis, total):
     new, columns = snapshots.shape
     modes = basis.shape[0]
-    width = blocks_of(columns, 2048)
-    steps = columns // width
+    width = blocks_of(columns, GRAM_WIDTH)
     count = new + modes
     return pl.pallas_call(
-        functools.partial(gram_kernel, 1.0 / total, steps),
+        functools.partial(gram_kernel, 1.0 / total, width),
         out_shape=jax.ShapeDtypeStruct((count, count), jnp.float32),
-        grid=(steps,),
-        in_specs=[
-            pl.BlockSpec((new, width), lambda i: (0, i)),
-            pl.BlockSpec((modes, width), lambda i: (0, i)),
+        in_specs=[pl.BlockSpec(memory_space=pltpu.HBM), pl.BlockSpec(memory_space=pltpu.HBM)],
+        out_specs=pl.BlockSpec(memory_space=pltpu.VMEM),
+        scratch_shapes=[
+            pltpu.VMEM((count, columns), jnp.float32),
+            pltpu.SemaphoreType.DMA((2, columns // width)),
         ],
-        out_specs=pl.BlockSpec((count, count), lambda i: (0, 0)),
-        scratch_shapes=[pltpu.VMEM((2 * count, 2 * count), jnp.float32)],
-        compiler_params=pltpu.CompilerParams(dimension_semantics=("arbitrary",)),
+        compiler_params=pltpu.CompilerParams(vmem_limit_bytes=GRANT),
         name="gram",
     )(snapshots, basis)
 
@@ -124,7 +127,7 @@
 
 
 def update_kernel(
-    width, sums_ref, sigma_ref, snap_ref, basis_ref, modes_ref, values_ref, data_ref, out_ref, step_ref, in_sem, out_sem
+    width, sums_ref, sigma_ref, snap_ref, basis_ref, modes_ref, values_ref, data_ref, out_ref, step_ref, frame_ref, in_sem, out_sem
 ):
     modes = basis_ref.shape[0]
     new, columns = snap_ref.shape
@@ -167,17 +170,17 @@
     step_ref[modes:, half : half + modes] = joined_t
     step_ref[modes:, half + modes : half + count] = residual
 
-    left = step_ref[:modes, :half]
-    right = step_ref[:modes, half:]
-    for step in range(ITERS):
-        if step:
-            both = dot(right[:, :count], step_ref[...])
-            left, right = both[:, :half], both[:, half:]
-        for repeat in range(2):
-            square = dot(left, right, NT)
-            left, right = normalize(square, [left, right])
-
-    after = dot(right[:, :count], step_ref[:, :half])
+    def once(repeat, parts):
+        return tuple(normalize(dot(*parts, NT), parts))
+
+    def iterate(step, parts):
+        left, right = lax.fori_loop(0, 2, once, parts)
+        frame_ref[...] = left
+        both = dot(right[:, :count], step_ref[...])
+        return both[:, :half], both[:, half:]
+
+    after, _ = lax.fori_loop(0, ITERS, iterate, (step_ref[:modes, :half], step_ref[:modes, half:]))
+    left = frame_ref[...]
     lane = lax.broadcasted_iota(jnp.int32, (modes, half), 1)
     spread = jnp.concatenate([sigma_row, jnp.zeros((1, half - modes), jnp.float32)], axis=1)
     part = jnp.where(lane < modes, left * spread, jnp.where(lane < count, after, 0.0))
@@ -222,17 +225,19 @@
         in_specs=[
             pl.BlockSpec(memory_space=pltpu.VMEM),
             pl.BlockSpec(memory_space=pltpu.VMEM),
-            pl.BlockSpec(memory_space=pl.ANY),
-            pl.BlockSpec(memory_space=pl.ANY),
+            pl.BlockSpec(memory_space=pltpu.HBM),
+            pl.BlockSpec(memory_space=pltpu.HBM),
         ],
-        out_specs=(pl.BlockSpec(memory_space=pl.ANY), pl.BlockSpec(memory_space=pltpu.VMEM)),
+        out_specs=(pl.BlockSpec(memory_space=pltpu.HBM), pl.BlockSpec(memory_space=pltpu.VMEM)),
         scratch_shapes=[
             pltpu.VMEM((count, columns), jnp.float32),
             pltpu.VMEM((modes, columns), jnp.float32),
             pltpu.VMEM((count, 2 * half), jnp.float32),
+            pltpu.VMEM((modes, half), jnp.float32),
             pltpu.SemaphoreType.DMA((2,)),
             pltpu.SemaphoreType.DMA((columns // width,)),
         ],
+        compiler_params=pltpu.CompilerParams(vmem_limit_bytes=GRANT),
         name="update",
     )(sums, sigma, snapshots, basis)
 
@@ -241,6 +246,8 @@
     total = basis.shape[1] * 1.0
     for _, size in sizes:
         total *= size
+    basis = pltpu.with_memory_space_constraint(basis, pltpu.HBM)
+    snapshots = pltpu.with_memory_space_constraint(snapshots, pltpu.HBM)
     sums = all_sum(gram(snapshots, basis, total), sizes)
     modes, values = update(sums, sigma.reshape(1, -1), snapshots, basis)
     return modes, values.reshape(-1)

time: 39.3 us -> 33.6 us (0.85)
  Pallas kernels: 16.6 us -> 12.5 us
  other arithmetic: 1.45 us -> 0.04 us
    pallas_call x1, Pallas kernels: 12.3 us -> 9.58 us  [update(): pl.pallas_call(functools.partial(update_kernel, width), out_shape=(jax.Sh...]
    add x5, other arithmetic: 1.45 us -> 0.04 us  [all_sum(): x = x + lax.ppermute(x, axis, [(i, i ^ bit) for i in range(size)])]
    pallas_call x1, Pallas kernels: 4.26 us -> 2.94 us  [gram(): pl.pallas_call(functools.partial(gram_kernel, 1.0 / total, width), out_sh...]
where the time goes in v3:
time: 33.6 us; the launch traced here: 33.4 us
  Pallas kernels  12.5 us (37%)
  starting transfers between devices  11 us (33%)
  waiting for transfers between devices  9.16 us (27%)
  between operations  0.66 us (2%)
    ppermute x5, starting transfers between devices, all_sum(): x = x + lax.ppermute(x, axis, [(i, i ^ bit) for i in range(size)])  11 us
    pallas_call x1, Pallas kernels, update(): pl.pallas_call(functools.partial(update_kernel, width), out_shape=(jax.Sh...  9.58 us
    ppermute x5, waiting for transfers between devices, all_sum(): x = x + lax.ppermute(x, axis, [(i, i ^ bit) for i in range(size)])  9.16 us
    pallas_call x1, Pallas kernels, gram(): pl.pallas_call(functools.partial(gram_kernel, 1.0 / total, width), out_sh...  2.94 us
  transfers between devices with their start and end apart: 5, of which 5 were waited for; matrix products, arithmetic and copies ran while one was open for 0% of the time, Pallas kernels for 0%

profile of v3, /device:TPU:0, one launch (start us, length us, event | category | flops | bytes accessed | tf_op | source)
XLA Modules:
  0.0 33.4 jit_solution(16468513903635188571)
XLA Ops:
  0.6 0.0 copy-start
  0.6 2.9 %gram.1 = f32[96,96]{1,0:T(8,128)S(1)} custom-call(f32[64,8192]{1,0:T(8,128)} %snap_ref.3, f32[32,8192]{1,0:T(8,128)} %basis_ref.3), custom_call_target="tpu_custom_call" | custom-call | tf_op jit(solution)/shard_map/gram/pallas_call | solution.py:66
  3.6 0.6 %collective-permute-start = (f32[96,96]{1,0:T(8,128)S(1)}, f32[96,96]{1,0:T(8,128)S(1)}, u32[]{:S(2)}, u32[]{:S(2)}) collective-permute-start(f32[96,96]{1,0:T(8,128)S(1)} %gram.1), channel_id=1, source_target_pairs={{0,16},{16,0},{1,17},{17,1},{2,18},{18,2},{3,19},{19,3},{4,20},{20... | collective-permute-start | bytes 110600 | tf_op jit(solution)/shard_map/ppermute | solution.py:87
  4.1 0.9 %collective-permute-done = f32[96,96]{1,0:T(8,128)S(1)} collective-permute-done((f32[96,96]{1,0:T(8,128)S(1)}, f32[96,96]{1,0:T(8,128)S(1)}, u32[]{:S(2)}, u32[]{:S(2)}) %collective-permute-start) | collective-permute-done | bytes 36896 | tf_op jit(solution)/shard_map/ppermute | solution.py:87
  5.0 2.9 %collective-permute-start.1 = (f32[96,96]{1,0:T(8,128)S(1)}, f32[96,96]{1,0:T(8,128)S(1)}, u32[]{:S(2)}, u32[]{:S(2)}) collective-permute-start(f32[96,96]{1,0:T(8,128)S(1)} %add.15), channel_id=1, source_target_pairs={{0,4},{4,0},{8,12},{12,8},{1,5},{5,1},{9,13},{13,9},{2,6},{6,2},{1... | collective-permute-start | bytes 110600 | tf_op jit(solution)/shard_map/ppermute | solution.py:87
  7.9 2.1 %collective-permute-done.1 = f32[96,96]{1,0:T(8,128)S(1)} collective-permute-done((f32[96,96]{1,0:T(8,128)S(1)}, f32[96,96]{1,0:T(8,128)S(1)}, u32[]{:S(2)}, u32[]{:S(2)}) %collective-permute-start.1) | collective-permute-done | bytes 36896 | tf_op jit(solution)/shard_map/ppermute | solution.py:87
  10.0 2.1 %collective-permute-start.2 = (f32[96,96]{1,0:T(8,128)S(1)}, f32[96,96]{1,0:T(8,128)S(1)}, u32[]{:S(2)}, u32[]{:S(2)}) collective-permute-start(f32[96,96]{1,0:T(8,128)S(1)} %add.16), channel_id=1, source_target_pairs={{0,8},{4,12},{8,0},{12,4},{1,9},{5,13},{9,1},{13,5},{2,10},{6,14},... | collective-permute-start | bytes 110600 | tf_op jit(solution)/shard_map/ppermute | solution.py:87
  12.1 2.1 %collective-permute-done.2 = f32[96,96]{1,0:T(8,128)S(1)} collective-permute-done((f32[96,96]{1,0:T(8,128)S(1)}, f32[96,96]{1,0:T(8,128)S(1)}, u32[]{:S(2)}, u32[]{:S(2)}) %collective-permute-start.2) | collective-permute-done | bytes 36896 | tf_op jit(solution)/shard_map/ppermute | solution.py:87
  14.2 2.1 %collective-permute-start.3 = (f32[96,96]{1,0:T(8,128)S(1)}, f32[96,96]{1,0:T(8,128)S(1)}, u32[]{:S(2)}, u32[]{:S(2)}) collective-permute-start(f32[96,96]{1,0:T(8,128)S(1)} %add.17), channel_id=1, source_target_pairs={{0,1},{1,0},{2,3},{3,2},{4,5},{5,4},{6,7},{7,6},{8,9},{9,8},{10,11... | collective-permute-start | bytes 110600 | tf_op jit(solution)/shard_map/ppermute | solution.py:87
  16.3 2.1 %collective-permute-done.3 = f32[96,96]{1,0:T(8,128)S(1)} collective-permute-done((f32[96,96]{1,0:T(8,128)S(1)}, f32[96,96]{1,0:T(8,128)S(1)}, u32[]{:S(2)}, u32[]{:S(2)}) %collective-permute-start.3) | collective-permute-done | bytes 36896 | tf_op jit(solution)/shard_map/ppermute | solution.py:87
  18.4 3.3 %collective-permute-start.4 = (f32[96,96]{1,0:T(8,128)S(1)}, f32[96,96]{1,0:T(8,128)S(1)}, u32[]{:S(2)}, u32[]{:S(2)}) collective-permute-start(f32[96,96]{1,0:T(8,128)S(1)} %add.18), channel_id=1, source_target_pairs={{0,2},{1,3},{2,0},{3,1},{4,6},{5,7},{6,4},{7,5},{8,10},{9,11},{10,... | collective-permute-start | bytes 110600 | tf_op jit(solution)/shard_map/ppermute | solution.py:87
  21.7 2.1 %collective-permute-done.4 = f32[96,96]{1,0:T(8,128)S(1)} collective-permute-done((f32[96,96]{1,0:T(8,128)S(1)}, f32[96,96]{1,0:T(8,128)S(1)}, u32[]{:S(2)}, u32[]{:S(2)}) %collective-permute-start.4) | collective-permute-done | bytes 36896 | tf_op jit(solution)/shard_map/ppermute | solution.py:87
  23.8 0.0 copy-done
  23.8 9.6 %update.1 = (f32[32,8192]{1,0:T(8,128)}, f32[1,32]{1,0:T(1,128)}) custom-call(f32[96,96]{1,0:T(8,128)S(1)} %add.19.sums_ref, f32[1,32]{1,0:T(1,128)S(1)} %bitcast.2, f32[64,8192]{1,0:T(8,128)} %snap_ref.3, f32[32,8192]{1,0:T(8,128)} %basis_ref.3), custom_call_target="tpu_custom_call" | custom-call | tf_op jit(solution)/shard_map/update/pallas_call | solution.py:219
  (5 shorter events, 0.0 us)
Async XLA Ops:
  0.6 23.2 %copy-start = (f32[32]{0:T(128)S(1)}, f32[32]{0:T(128)}, u32[]{:S(2)}) copy-start(f32[32]{0:T(128)} %param.4) | copy-start | bytes 388
  3.6 1.4 %collective-permute-start = (f32[96,96]{1,0:T(8,128)S(1)}, f32[96,96]{1,0:T(8,128)S(1)}, u32[]{:S(2)}, u32[]{:S(2)}) collective-permute-start(f32[96,96]{1,0:T(8,128)S(1)} %gram.1), channel_id=1, source_target_pairs={{0,16},{16,0},{1,17},{17,1},{2,18},{18,2},{3,19},{19,3},{4,20},{20... | collective-permute-start | bytes 110600 | tf_op jit(solution)/shard_map/ppermute | solution.py:87
  5.0 5.0 %collective-permute-start.1 = (f32[96,96]{1,0:T(8,128)S(1)}, f32[96,96]{1,0:T(8,128)S(1)}, u32[]{:S(2)}, u32[]{:S(2)}) collective-permute-start(f32[96,96]{1,0:T(8,128)S(1)} %add.15), channel_id=1, source_target_pairs={{0,4},{4,0},{8,12},{12,8},{1,5},{5,1},{9,13},{13,9},{2,6},{6,2},{1... | collective-permute-start | bytes 110600 | tf_op jit(solution)/shard_map/ppermute | solution.py:87
  10.0 4.2 %collective-permute-start.2 = (f32[96,96]{1,0:T(8,128)S(1)}, f32[96,96]{1,0:T(8,128)S(1)}, u32[]{:S(2)}, u32[]{:S(2)}) collective-permute-start(f32[96,96]{1,0:T(8,128)S(1)} %add.16), channel_id=1, source_target_pairs={{0,8},{4,12},{8,0},{12,4},{1,9},{5,13},{9,1},{13,5},{2,10},{6,14},... | collective-permute-start | bytes 110600 | tf_op jit(solution)/shard_map/ppermute | solution.py:87
  14.2 4.2 %collective-permute-start.3 = (f32[96,96]{1,0:T(8,128)S(1)}, f32[96,96]{1,0:T(8,128)S(1)}, u32[]{:S(2)}, u32[]{:S(2)}) collective-permute-start(f32[96,96]{1,0:T(8,128)S(1)} %add.17), channel_id=1, source_target_pairs={{0,1},{1,0},{2,3},{3,2},{4,5},{5,4},{6,7},{7,6},{8,9},{9,8},{10,11... | collective-permute-start | bytes 110600 | tf_op jit(solution)/shard_map/ppermute | solution.py:87
  18.4 5.4 %collective-permute-start.4 = (f32[96,96]{1,0:T(8,128)S(1)}, f32[96,96]{1,0:T(8,128)S(1)}, u32[]{:S(2)}, u32[]{:S(2)}) collective-permute-start(f32[96,96]{1,0:T(8,128)S(1)} %add.18), channel_id=1, source_target_pairs={{0,2},{1,3},{2,0},{3,1},{4,6},{5,7},{6,4},{7,5},{8,10},{9,11},{10,... | collective-permute-start | bytes 110600 | tf_op jit(solution)/shard_map/ppermute | solution.py:87

commit v4 on v3

--- a/solution.py
+++ b/solution.py
@@ -108,20 +108,21 @@
         pivot = jnp.broadcast_to(column[own][r : r + 1], (8, lanes))
         pivots[own] = jnp.where(row == r, pivot, pivots[own])
         inverse = 1.0 / pivot
+        scaled = [None if c is None else c * inverse for c in column]
         for l in range(k + 1, n):
             entry = jnp.broadcast_to(column[l // 8][l % 8 : l % 8 + 1], (8, lanes))
             for q in range(l // 8, groups):
                 if l == k + 1:
                     spread[l][q] = spread[l][q] - (column[q] * entry) * inverse
                 else:
-                    spread[l][q] = spread[l][q] - column[q] * (entry * inverse)
+                    spread[l][q] = spread[l][q] - scaled[q] * entry
+        below = jnp.where(row > r, scaled[own], 0.0)
         for p in parts:
-            line = jnp.broadcast_to(p[own][r : r + 1], (8, lanes)) * inverse
-            for q in range(own, groups):
-                if q > own:
-                    p[q] = p[q] - column[q] * line
-                elif r < 7:
-                    p[q] = p[q] - jnp.where(row > r, column[q], 0.0) * line
+            line = jnp.broadcast_to(p[own][r : r + 1], (8, lanes))
+            if r < 7:
+                p[own] = p[own] - below * line
+            for q in range(own + 1, groups):
+                p[q] = p[q] - scaled[q] * line
     scales = [lax.rsqrt(p) for p in pivots]
     return [jnp.concatenate([x * s for x, s in zip(p, scales)], axis=0) for p in parts]
 
@@ -139,73 +140,65 @@
     for load in loads:
         load.start()
 
-    gram_all = sums_ref[...]
-    snap_gram = gram_all[:new, :new]
-    first_t = gram_all[:new, new:]
-    first = gram_all[new:, :new]
-    corr = gram_all[new:, new:]
-    joined = 2.0 * first - dot(corr, first)
-    joined_t = 2.0 * first_t - dot(first_t, corr)
-    rest = first_t - dot(joined_t, corr)
-    residual = snap_gram - dot(joined_t, first) - dot(rest, joined)
-    eye = (
-        lax.broadcasted_iota(jnp.int32, (modes, modes), 0) == lax.broadcasted_iota(jnp.int32, (modes, modes), 1)
-    )
-    sigma_row = sigma_ref[...]
-    sigma2 = sigma_row * sigma_row
-    corner = jnp.where(eye, sigma2, 0.0) + dot(joined, joined_t)
-    bend = dot(joined, residual)
-    eye_new = (
-        lax.broadcasted_iota(jnp.int32, (new, new), 0) == lax.broadcasted_iota(jnp.int32, (new, new), 1)
-    ).astype(jnp.float32)
-
     half = step_ref.shape[1] // 2
-    step_ref[...] = jnp.zeros_like(step_ref)
-    step_ref[:modes, :modes] = corner
-    step_ref[:modes, modes:count] = joined
-    step_ref[:modes, half : half + modes] = corner
-    step_ref[:modes, half + modes : half + count] = bend
-    step_ref[modes:, :modes] = joined_t
-    step_ref[modes:, modes:count] = eye_new
-    step_ref[modes:, half : half + modes] = joined_t
-    step_ref[modes:, half + modes : half + count] = residual
-
-    def once(repeat, parts):
-        return tuple(normalize(dot(*parts, NT), parts))
+    top = sums_ref[:new]
+    low = sums_ref[new:]
+    lane = lax.broadcasted_iota(jnp.int32, (modes, count), 1)
+    on_modes = lane >= new
+    diagonal = lane == new + lax.broadcasted_iota(jnp.int32, (modes, count), 0)
+    wide = lax.broadcasted_iota(jnp.int32, (new, count), 1)
+    unit = (wide == lax.broadcasted_iota(jnp.int32, (new, count), 0)).astype(jnp.float32)
+    sigma = jnp.concatenate([jnp.zeros((1, new), jnp.float32), sigma_ref[...]], axis=1)
+
+    def below(x):
+        return jnp.concatenate([jnp.zeros((new, count), jnp.float32), x], axis=0)
+
+    corr = jnp.where(on_modes, low, 0.0)
+    twice = jnp.where(diagonal, 2.0, 0.0) - corr
+    first = jnp.where(on_modes, 0.0, low)
+    joined_t = dot(top, below(twice), NT)
+    joined = dot(twice, below(first))
+    rest = jnp.where(wide >= new, top, 0.0) - dot(joined_t, below(corr), NT)
+    corner = jnp.where(diagonal, sigma * sigma, 0.0) + dot(joined, below(joined), NT)
+    residual = jnp.where(wide >= new, 0.0, top) - dot(joined_t, below(first)) - dot(rest, below(joined))
+    bend = dot(joined[:, :new], residual)
+
+    step_ref[:, count:half] = jnp.zeros((count, half - count), jnp.float32)
+    step_ref[:, half + count :] = jnp.zeros((count, half - count), jnp.float32)
+    step_ref[:new, :count] = unit + joined_t
+    step_ref[new:, :count] = joined + corner
+    step_ref[:new, half : half + count] = residual + joined_t
+    step_ref[new:, half : half + count] = bend + corner
 
     def iterate(step, parts):
-        left, right = lax.fori_loop(0, 2, once, parts)
+        left, right = normalize(dot(*parts, NT), parts)
+        after = dot(right[:, :count], step_ref[...])
+        left, *after = normalize(dot(left, right, NT), [left, after[:, :half], after[:, half:]])
         frame_ref[...] = left
-        both = dot(right[:, :count], step_ref[...])
-        return both[:, :half], both[:, half:]
-
-    after, _ = lax.fori_loop(0, ITERS, iterate, (step_ref[:modes, :half], step_ref[:modes, half:]))
-    left = frame_ref[...]
-    lane = lax.broadcasted_iota(jnp.int32, (modes, half), 1)
-    spread = jnp.concatenate([sigma_row, jnp.zeros((1, half - modes), jnp.float32)], axis=1)
-    part = jnp.where(lane < modes, left * spread, jnp.where(lane < count, after, 0.0))
-    ritz = dot(jnp.ones((8, half), jnp.float32), part * part, NT)
-    values_ref[...] = jnp.sqrt(ritz[:1])
-
-    y = left[:, :modes]
-    z = left[:, modes:count]
-    weights = jnp.concatenate([z, y - dot(z, joined_t)], axis=1)
-    high, low = split(weights)
+        return tuple(after)
+
+    after, _ = lax.fori_loop(0, ITERS, iterate, (step_ref[new:, :half], step_ref[new:, half:]))
+    left = frame_ref[:, :count]
+
+    weights = left - dot(left[:, :new], joined_t)
+    high, low_part = split(weights)
     left_side = jnp.concatenate(
-        [jnp.concatenate([high, high], axis=1), jnp.concatenate([low, low], axis=1)], axis=0
+        [jnp.concatenate([high, high], axis=1), jnp.concatenate([low_part, low_part], axis=1)], axis=0
     )
     for load in loads:
         load.wait()
     stores = []
     for i in range(columns // width):
         piece = pl.ds(i * width, width)
-        data_high, data_low = split(data_ref[:, piece])
-        data = jnp.concatenate([data_high, data_low], axis=0)
+        data = jnp.concatenate(split(data_ref[:, piece]), axis=0)
         product = lax.dot_general(left_side, data, NN, preferred_element_type=jnp.float32)
         out_ref[:, piece] = product[:modes] + product[modes:]
         store = pltpu.make_async_copy(out_ref.at[:, piece], modes_ref.at[:, piece], out_sem.at[i])
         store.start()
         stores.append(store)
+
+    part = jnp.where(on_modes, left * sigma, after[:, :count])
+    values_ref[...] = jnp.sqrt(dot(jnp.ones((8, count), jnp.float32), part * part, NT)[:1])
     for store in stores:
         store.wait()
 

time: 33.6 us -> 32.9 us (0.979)
  Pallas kernels: 12.5 us -> 11.9 us
    pallas_call x1, Pallas kernels: 9.58 us -> 8.93 us  [update(): pl.pallas_call(functools.partial(update_kernel, width), out_shape=(jax.Sh...]
where the time goes in v4:
time: 32.9 us; the launch traced here: 32.8 us
  Pallas kernels  11.9 us (36%)
  starting transfers between devices  11 us (33%)
  waiting for transfers between devices  9.16 us (28%)
  between operations  0.66 us (2%)
    ppermute x5, starting transfers between devices, all_sum(): x = x + lax.ppermute(x, axis, [(i, i ^ bit) for i in range(size)])  11 us
    ppermute x5, waiting for transfers between devices, all_sum(): x = x + lax.ppermute(x, axis, [(i, i ^ bit) for i in range(size)])  9.16 us
    pallas_call x1, Pallas kernels, update(): pl.pallas_call(functools.partial(update_kernel, width), out_shape=(jax.Sh...  8.93 us
    pallas_call x1, Pallas kernels, gram(): pl.pallas_call(functools.partial(gram_kernel, 1.0 / total, width), out_sh...  2.94 us
  transfers between devices with their start and end apart: 5, of which 5 were waited for; matrix products, arithmetic and copies ran while one was open for 0% of the time, Pallas kernels for 0%

profile of v4, /device:TPU:0, one launch (start us, length us, event | category | flops | bytes accessed | tf_op | source)
XLA Modules:
  0.0 32.8 jit_solution(10073257421488914986)
XLA Ops:
  0.6 0.0 copy-start
  0.6 2.9 %gram.1 = f32[96,96]{1,0:T(8,128)S(1)} custom-call(f32[64,8192]{1,0:T(8,128)} %snap_ref.3, f32[32,8192]{1,0:T(8,128)} %basis_ref.3), custom_call_target="tpu_custom_call" | custom-call | tf_op jit(solution)/shard_map/gram/pallas_call | solution.py:66
  3.6 0.6 %collective-permute-start = (f32[96,96]{1,0:T(8,128)S(1)}, f32[96,96]{1,0:T(8,128)S(1)}, u32[]{:S(2)}, u32[]{:S(2)}) collective-permute-start(f32[96,96]{1,0:T(8,128)S(1)} %gram.1), channel_id=1, source_target_pairs={{0,16},{16,0},{1,17},{17,1},{2,18},{18,2},{3,19},{19,3},{4,20},{20... | collective-permute-start | bytes 110600 | tf_op jit(solution)/shard_map/ppermute | solution.py:87
  4.1 0.9 %collective-permute-done = f32[96,96]{1,0:T(8,128)S(1)} collective-permute-done((f32[96,96]{1,0:T(8,128)S(1)}, f32[96,96]{1,0:T(8,128)S(1)}, u32[]{:S(2)}, u32[]{:S(2)}) %collective-permute-start) | collective-permute-done | bytes 36896 | tf_op jit(solution)/shard_map/ppermute | solution.py:87
  5.0 2.9 %collective-permute-start.1 = (f32[96,96]{1,0:T(8,128)S(1)}, f32[96,96]{1,0:T(8,128)S(1)}, u32[]{:S(2)}, u32[]{:S(2)}) collective-permute-start(f32[96,96]{1,0:T(8,128)S(1)} %add.15), channel_id=1, source_target_pairs={{0,4},{4,0},{8,12},{12,8},{1,5},{5,1},{9,13},{13,9},{2,6},{6,2},{1... | collective-permute-start | bytes 110600 | tf_op jit(solution)/shard_map/ppermute | solution.py:87
  7.9 2.1 %collective-permute-done.1 = f32[96,96]{1,0:T(8,128)S(1)} collective-permute-done((f32[96,96]{1,0:T(8,128)S(1)}, f32[96,96]{1,0:T(8,128)S(1)}, u32[]{:S(2)}, u32[]{:S(2)}) %collective-permute-start.1) | collective-permute-done | bytes 36896 | tf_op jit(solution)/shard_map/ppermute | solution.py:87
  10.0 2.1 %collective-permute-start.2 = (f32[96,96]{1,0:T(8,128)S(1)}, f32[96,96]{1,0:T(8,128)S(1)}, u32[]{:S(2)}, u32[]{:S(2)}) collective-permute-start(f32[96,96]{1,0:T(8,128)S(1)} %add.16), channel_id=1, source_target_pairs={{0,8},{4,12},{8,0},{12,4},{1,9},{5,13},{9,1},{13,5},{2,10},{6,14},... | collective-permute-start | bytes 110600 | tf_op jit(solution)/shard_map/ppermute | solution.py:87
  12.1 2.1 %collective-permute-done.2 = f32[96,96]{1,0:T(8,128)S(1)} collective-permute-done((f32[96,96]{1,0:T(8,128)S(1)}, f32[96,96]{1,0:T(8,128)S(1)}, u32[]{:S(2)}, u32[]{:S(2)}) %collective-permute-start.2) | collective-permute-done | bytes 36896 | tf_op jit(solution)/shard_map/ppermute | solution.py:87
  14.2 2.1 %collective-permute-start.3 = (f32[96,96]{1,0:T(8,128)S(1)}, f32[96,96]{1,0:T(8,128)S(1)}, u32[]{:S(2)}, u32[]{:S(2)}) collective-permute-start(f32[96,96]{1,0:T(8,128)S(1)} %add.17), channel_id=1, source_target_pairs={{0,1},{1,0},{2,3},{3,2},{4,5},{5,4},{6,7},{7,6},{8,9},{9,8},{10,11... | collective-permute-start | bytes 110600 | tf_op jit(solution)/shard_map/ppermute | solution.py:87
  16.3 2.1 %collective-permute-done.3 = f32[96,96]{1,0:T(8,128)S(1)} collective-permute-done((f32[96,96]{1,0:T(8,128)S(1)}, f32[96,96]{1,0:T(8,128)S(1)}, u32[]{:S(2)}, u32[]{:S(2)}) %collective-permute-start.3) | collective-permute-done | bytes 36896 | tf_op jit(solution)/shard_map/ppermute | solution.py:87
  18.4 3.3 %collective-permute-start.4 = (f32[96,96]{1,0:T(8,128)S(1)}, f32[96,96]{1,0:T(8,128)S(1)}, u32[]{:S(2)}, u32[]{:S(2)}) collective-permute-start(f32[96,96]{1,0:T(8,128)S(1)} %add.18), channel_id=1, source_target_pairs={{0,2},{1,3},{2,0},{3,1},{4,6},{5,7},{6,4},{7,5},{8,10},{9,11},{10,... | collective-permute-start | bytes 110600 | tf_op jit(solution)/shard_map/ppermute | solution.py:87
  21.7 2.1 %collective-permute-done.4 = f32[96,96]{1,0:T(8,128)S(1)} collective-permute-done((f32[96,96]{1,0:T(8,128)S(1)}, f32[96,96]{1,0:T(8,128)S(1)}, u32[]{:S(2)}, u32[]{:S(2)}) %collective-permute-start.4) | collective-permute-done | bytes 36896 | tf_op jit(solution)/shard_map/ppermute | solution.py:87
  23.8 0.0 copy-done
  23.8 8.9 %update.1 = (f32[32,8192]{1,0:T(8,128)}, f32[1,32]{1,0:T(1,128)}) custom-call(f32[96,96]{1,0:T(8,128)S(1)} %add.19.sums_ref, f32[1,32]{1,0:T(1,128)S(1)} %bitcast.2, f32[64,8192]{1,0:T(8,128)} %snap_ref.3, f32[32,8192]{1,0:T(8,128)} %basis_ref.3), custom_call_target="tpu_custom_call" | custom-call | tf_op jit(solution)/shard_map/update/pallas_call | solution.py:212
  (5 shorter events, 0.0 us)
Async XLA Ops:
  0.6 23.2 %copy-start = (f32[32]{0:T(128)S(1)}, f32[32]{0:T(128)}, u32[]{:S(2)}) copy-start(f32[32]{0:T(128)} %param.4) | copy-start | bytes 388
  3.6 1.4 %collective-permute-start = (f32[96,96]{1,0:T(8,128)S(1)}, f32[96,96]{1,0:T(8,128)S(1)}, u32[]{:S(2)}, u32[]{:S(2)}) collective-permute-start(f32[96,96]{1,0:T(8,128)S(1)} %gram.1), channel_id=1, source_target_pairs={{0,16},{16,0},{1,17},{17,1},{2,18},{18,2},{3,19},{19,3},{4,20},{20... | collective-permute-start | bytes 110600 | tf_op jit(solution)/shard_map/ppermute | solution.py:87
  5.0 5.0 %collective-permute-start.1 = (f32[96,96]{1,0:T(8,128)S(1)}, f32[96,96]{1,0:T(8,128)S(1)}, u32[]{:S(2)}, u32[]{:S(2)}) collective-permute-start(f32[96,96]{1,0:T(8,128)S(1)} %add.15), channel_id=1, source_target_pairs={{0,4},{4,0},{8,12},{12,8},{1,5},{5,1},{9,13},{13,9},{2,6},{6,2},{1... | collective-permute-start | bytes 110600 | tf_op jit(solution)/shard_map/ppermute | solution.py:87
  10.0 4.2 %collective-permute-start.2 = (f32[96,96]{1,0:T(8,128)S(1)}, f32[96,96]{1,0:T(8,128)S(1)}, u32[]{:S(2)}, u32[]{:S(2)}) collective-permute-start(f32[96,96]{1,0:T(8,128)S(1)} %add.16), channel_id=1, source_target_pairs={{0,8},{4,12},{8,0},{12,4},{1,9},{5,13},{9,1},{13,5},{2,10},{6,14},... | collective-permute-start | bytes 110600 | tf_op jit(solution)/shard_map/ppermute | solution.py:87
  14.2 4.2 %collective-permute-start.3 = (f32[96,96]{1,0:T(8,128)S(1)}, f32[96,96]{1,0:T(8,128)S(1)}, u32[]{:S(2)}, u32[]{:S(2)}) collective-permute-start(f32[96,96]{1,0:T(8,128)S(1)} %add.17), channel_id=1, source_target_pairs={{0,1},{1,0},{2,3},{3,2},{4,5},{5,4},{6,7},{7,6},{8,9},{9,8},{10,11... | collective-permute-start | bytes 110600 | tf_op jit(solution)/shard_map/ppermute | solution.py:87
  18.4 5.4 %collective-permute-start.4 = (f32[96,96]{1,0:T(8,128)S(1)}, f32[96,96]{1,0:T(8,128)S(1)}, u32[]{:S(2)}, u32[]{:S(2)}) collective-permute-start(f32[96,96]{1,0:T(8,128)S(1)} %add.18), channel_id=1, source_target_pairs={{0,2},{1,3},{2,0},{3,1},{4,6},{5,7},{6,4},{7,5},{8,10},{9,11},{10,... | collective-permute-start | bytes 110600 | tf_op jit(solution)/shard_map/ppermute | solution.py:87

commit v5 on v4

--- a/solution.py
+++ b/solution.py
@@ -11,13 +11,33 @@
 GRAM_WIDTH = 4096
 GRANT = 24 * 1024 * 1024
 AXES = ("gx", "gy", "gz")
-HIGH = lax.Precision.HIGHEST
 NN = (((1,), (0,)), ((), ()))
 NT = (((1,), (1,)), ((), ()))
 
 
+def pieces(x):
+    high = x.astype(jnp.bfloat16)
+    rest = x - high.astype(jnp.float32)
+    middle = rest.astype(jnp.bfloat16)
+    return high, middle, (rest - middle.astype(jnp.float32)).astype(jnp.bfloat16)
+
+
+def as_left(x):
+    high, middle, low = pieces(x)
+    return jnp.concatenate([high, middle, high, low, middle, high], axis=1)
+
+
+def as_right(x, axis):
+    high, middle, low = pieces(x)
+    return jnp.concatenate([high, high, middle, high, middle, low], axis=axis)
+
+
+def product_of(left, right, dims=NN):
+    return lax.dot_general(left, right, dims, preferred_element_type=jnp.float32)
+
+
 def dot(a, b, dims=NN):
-    return lax.dot_general(a, b, dims, precision=HIGH, preferred_element_type=jnp.float32)
+    return product_of(as_left(a), as_right(b, dims[0][1][0]), dims)
 
 
 def split(x):
@@ -51,11 +71,16 @@
     for i in range(steps):
         for load in loads[i]:
             load.wait()
-        both = jnp.concatenate(split(data_ref[:, pl.ds(i * width, width)]), axis=0)
-        product = lax.dot_general(both, both, NT, preferred_element_type=jnp.float32)
+        piece = pl.ds(i * width, width)
+        snap, basis = split(data_ref[:new, piece]), split(data_ref[new:, piece])
+        rows = jnp.concatenate([snap[0], basis[0], snap[1], basis[1]], axis=0)
+        product = product_of(rows, rows, NT)
         total = product if total is None else total + product
-    rows = total[:count] + total[count:]
-    out_ref[...] = (rows[:, :count] + rows[:, count:]) * scale
+    sent = out_ref.shape[1]
+    rows = (total[:count] + total[count:]) * scale
+    rows = rows[:, :count] + rows[:, count:]
+    corr = jnp.concatenate([rows[new:, new:], jnp.zeros((new - modes, modes), jnp.float32)], axis=0)
+    out_ref[...] = jnp.concatenate([rows[:new], corr], axis=1)
 
 
 def gram(snapshots, basis, total):
@@ -65,7 +90,7 @@
     count = new + modes
     return pl.pallas_call(
         functools.partial(gram_kernel, 1.0 / total, width),
-        out_shape=jax.ShapeDtypeStruct((count, count), jnp.float32),
+        out_shape=jax.ShapeDtypeStruct((new, count + modes), jnp.float32),
         in_specs=[pl.BlockSpec(memory_space=pltpu.HBM), pl.BlockSpec(memory_space=pltpu.HBM)],
         out_specs=pl.BlockSpec(memory_space=pltpu.VMEM),
         scratch_shapes=[
@@ -140,47 +165,59 @@
     for load in loads:
         load.start()
 
-    half = step_ref.shape[1] // 2
-    top = sums_ref[:new]
-    low = sums_ref[new:]
-    lane = lax.broadcasted_iota(jnp.int32, (modes, count), 1)
-    on_modes = lane >= new
-    diagonal = lane == new + lax.broadcasted_iota(jnp.int32, (modes, count), 0)
-    wide = lax.broadcasted_iota(jnp.int32, (new, count), 1)
-    unit = (wide == lax.broadcasted_iota(jnp.int32, (new, count), 0)).astype(jnp.float32)
-    sigma = jnp.concatenate([jnp.zeros((1, new), jnp.float32), sigma_ref[...]], axis=1)
-
-    def below(x):
-        return jnp.concatenate([jnp.zeros((new, count), jnp.float32), x], axis=0)
-
-    corr = jnp.where(on_modes, low, 0.0)
-    twice = jnp.where(diagonal, 2.0, 0.0) - corr
-    first = jnp.where(on_modes, 0.0, low)
-    joined_t = dot(top, below(twice), NT)
-    joined = dot(twice, below(first))
-    rest = jnp.where(wide >= new, top, 0.0) - dot(joined_t, below(corr), NT)
-    corner = jnp.where(diagonal, sigma * sigma, 0.0) + dot(joined, below(joined), NT)
-    residual = jnp.where(wide >= new, 0.0, top) - dot(joined_t, below(first)) - dot(rest, below(joined))
-    bend = dot(joined[:, :new], residual)
-
-    step_ref[:, count:half] = jnp.zeros((count, half - count), jnp.float32)
-    step_ref[:, half + count :] = jnp.zeros((count, half - count), jnp.float32)
-    step_ref[:new, :count] = unit + joined_t
-    step_ref[new:, :count] = joined + corner
-    step_ref[:new, half : half + count] = residual + joined_t
-    step_ref[new:, half : half + count] = bend + corner
-
-    def iterate(step, parts):
+    half = sums_ref.shape[1]
+    top = sums_ref[...]
+    lane = lax.broadcasted_iota(jnp.int32, (modes, half), 1)
+    line = lax.broadcasted_iota(jnp.int32, (modes, half), 0)
+    wide = lax.broadcasted_iota(jnp.int32, (new, half), 1)
+    unit = (wide == lax.broadcasted_iota(jnp.int32, (new, half), 0)).astype(jnp.float32)
+    sigma = jnp.concatenate(
+        [jnp.zeros((1, new), jnp.float32), sigma_ref[...], jnp.zeros((1, half - count), jnp.float32)], axis=1
+    )
+
+    def at(place, x):
+        above = [jnp.zeros((place, x.shape[1]), x.dtype)] if place else []
+        under = half - place - x.shape[0]
+        return jnp.concatenate(above + [x] + ([jnp.zeros((under, x.shape[1]), x.dtype)] if under else []), axis=0)
+
+    corr = jnp.where(lane >= count, top[:modes], 0.0)
+    same = jnp.where(lane == count + line, 1.0, 0.0)
+    twice = 2.0 * same - corr
+    pair = dot(jnp.where(wide < count, top, 0.0), at(new, jnp.concatenate([twice, same], axis=1)))
+    joined_t, first_t = pair[:, :half], pair[:, half:]
+    joined = dot(twice, at(0, first_t), NT)
+    joined_at = dot(first_t, at(new, twice), NT)
+    rest = first_t - dot(joined_t, at(count, corr))
+    residual = (
+        jnp.where(wide < new, top, 0.0) - dot(joined_t, at(0, first_t), NT) - dot(rest, at(0, joined_t), NT)
+    )
+    corner = jnp.where(lane == new + line, sigma * sigma, 0.0) + dot(joined, at(new, joined), NT)
+    bend = dot(joined, at(0, residual))
+
+    step = jnp.concatenate(
+        [
+            at(0, unit + joined_at) + at(new, joined + corner),
+            at(0, residual + joined_at) + at(new, bend + corner),
+        ],
+        axis=1,
+    )
+    step_ref[...] = as_right(step, 0)
+
+    def iterate(_, parts):
         left, right = normalize(dot(*parts, NT), parts)
-        after = dot(right[:, :count], step_ref[...])
-        left, *after = normalize(dot(left, right, NT), [left, after[:, :half], after[:, half:]])
+        right = as_left(right)
+        after = product_of(right, step_ref[...])
+        high, middle, last = right[:, :half], right[:, half : 2 * half], right[:, 3 * half : 4 * half]
+        square = product_of(as_left(left), jnp.concatenate([high, high, middle, high, middle, last], axis=1), NT)
+        left, *after = normalize(square, [left, after[:, :half], after[:, half:]])
         frame_ref[...] = left
         return tuple(after)
 
-    after, _ = lax.fori_loop(0, ITERS, iterate, (step_ref[new:, :half], step_ref[new:, half:]))
-    left = frame_ref[:, :count]
-
-    weights = left - dot(left[:, :new], joined_t)
+    start = (joined + corner, bend + corner)
+    after, _ = lax.fori_loop(0, ITERS, iterate, start)
+    left = frame_ref[...]
+
+    weights = (left - dot(left, at(0, joined_at)))[:, :count]
     high, low_part = split(weights)
     left_side = jnp.concatenate(
         [jnp.concatenate([high, high], axis=1), jnp.concatenate([low_part, low_part], axis=1)], axis=0
@@ -197,8 +234,8 @@
         store.start()
         stores.append(store)
 
-    part = jnp.where(on_modes, left * sigma, after[:, :count])
-    values_ref[...] = jnp.sqrt(dot(jnp.ones((8, count), jnp.float32), part * part, NT)[:1])
+    part = jnp.where(lane < new, after, left * sigma)
+    values_ref[...] = jnp.sqrt(dot(jnp.ones((8, half), jnp.float32), part * part, NT)[:1])
     for store in stores:
         store.wait()
 
@@ -208,7 +245,7 @@
     modes = basis.shape[0]
     count = new + modes
     width = blocks_of(columns, 2048)
-    half = -(-count // 128) * 128
+    half = count + modes
     return pl.pallas_call(
         functools.partial(update_kernel, width),
         out_shape=(
@@ -225,7 +262,7 @@
         scratch_shapes=[
             pltpu.VMEM((count, columns), jnp.float32),
             pltpu.VMEM((modes, columns), jnp.float32),
-            pltpu.VMEM((count, 2 * half), jnp.float32),
+            pltpu.VMEM((6 * half, 2 * half), jnp.bfloat16),
             pltpu.VMEM((modes, half), jnp.float32),
             pltpu.SemaphoreType.DMA((2,)),
             pltpu.SemaphoreType.DMA((columns // width,)),

time: 32.9 us -> 31.4 us (0.954)
  waiting for transfers between devices: 9.16 us -> 8.43 us
  starting transfers between devices: 11 us -> 10.5 us
    ppermute x5, waiting for transfers between devices: 9.16 us -> 8.43 us  [all_sum(): x = x + lax.ppermute(x, axis, [(i, i ^ bit) for i in range(size)])]
    ppermute x5, starting transfers between devices: 11 us -> 10.5 us  [all_sum(): x = x + lax.ppermute(x, axis, [(i, i ^ bit) for i in range(size)])]
    pallas_call x1, Pallas kernels: 8.93 us -> 8.6 us  [update(): pl.pallas_call(functools.partial(update_kernel, width), out_shape=(jax.Sh...]
where the time goes in v5:
time: 31.4 us; the launch traced here: 31.3 us
  Pallas kernels  11.6 us (37%)
  starting transfers between devices  10.5 us (33%)
  waiting for transfers between devices  8.43 us (27%)
  between operations  0.66 us (2%)
    ppermute x5, starting transfers between devices, all_sum(): x = x + lax.ppermute(x, axis, [(i, i ^ bit) for i in range(size)])  10.5 us
    pallas_call x1, Pallas kernels, update(): pl.pallas_call(functools.partial(update_kernel, width), out_shape=(jax.Sh...  8.6 us
    ppermute x5, waiting for transfers between devices, all_sum(): x = x + lax.ppermute(x, axis, [(i, i ^ bit) for i in range(size)])  8.43 us
    pallas_call x1, Pallas kernels, gram(): pl.pallas_call(functools.partial(gram_kernel, 1.0 / total, width), out_sh...  3.01 us
  transfers between devices with their start and end apart: 5, of which 5 were waited for; matrix products, arithmetic and copies ran while one was open for 0% of the time, Pallas kernels for 0%

profile of v5, /device:TPU:0, one launch (start us, length us, event | category | flops | bytes accessed | tf_op | source)
XLA Modules:
  0.0 31.3 jit_solution(7543128298805464719)
XLA Ops:
  0.6 0.0 copy-start
  0.6 3.0 %gram.1 = f32[64,128]{1,0:T(8,128)S(1)} custom-call(f32[64,8192]{1,0:T(8,128)} %snap_ref.3, f32[32,8192]{1,0:T(8,128)} %basis_ref.3), custom_call_target="tpu_custom_call" | custom-call | tf_op jit(solution)/shard_map/gram/pallas_call | solution.py:91
  3.7 0.6 %collective-permute-start = (f32[64,128]{1,0:T(8,128)S(1)}, f32[64,128]{1,0:T(8,128)S(1)}, u32[]{:S(2)}, u32[]{:S(2)}) collective-permute-start(f32[64,128]{1,0:T(8,128)S(1)} %gram.1), channel_id=1, source_target_pairs={{0,16},{16,0},{1,17},{17,1},{2,18},{18,2},{3,19},{19,3},{4,20},{20... | collective-permute-start | bytes 98312 | tf_op jit(solution)/shard_map/ppermute | solution.py:112
  4.2 0.9 %collective-permute-done = f32[64,128]{1,0:T(8,128)S(1)} collective-permute-done((f32[64,128]{1,0:T(8,128)S(1)}, f32[64,128]{1,0:T(8,128)S(1)}, u32[]{:S(2)}, u32[]{:S(2)}) %collective-permute-start) | collective-permute-done | bytes 32800 | tf_op jit(solution)/shard_map/ppermute | solution.py:112
  5.1 2.8 %collective-permute-start.1 = (f32[64,128]{1,0:T(8,128)S(1)}, f32[64,128]{1,0:T(8,128)S(1)}, u32[]{:S(2)}, u32[]{:S(2)}) collective-permute-start(f32[64,128]{1,0:T(8,128)S(1)} %add.15), channel_id=1, source_target_pairs={{0,4},{4,0},{8,12},{12,8},{1,5},{5,1},{9,13},{13,9},{2,6},{6,2},{1... | collective-permute-start | bytes 98312 | tf_op jit(solution)/shard_map/ppermute | solution.py:112
  7.9 1.9 %collective-permute-done.1 = f32[64,128]{1,0:T(8,128)S(1)} collective-permute-done((f32[64,128]{1,0:T(8,128)S(1)}, f32[64,128]{1,0:T(8,128)S(1)}, u32[]{:S(2)}, u32[]{:S(2)}) %collective-permute-start.1) | collective-permute-done | bytes 32800 | tf_op jit(solution)/shard_map/ppermute | solution.py:112
  9.8 2.1 %collective-permute-start.2 = (f32[64,128]{1,0:T(8,128)S(1)}, f32[64,128]{1,0:T(8,128)S(1)}, u32[]{:S(2)}, u32[]{:S(2)}) collective-permute-start(f32[64,128]{1,0:T(8,128)S(1)} %add.16), channel_id=1, source_target_pairs={{0,8},{4,12},{8,0},{12,4},{1,9},{5,13},{9,1},{13,5},{2,10},{6,14},... | collective-permute-start | bytes 98312 | tf_op jit(solution)/shard_map/ppermute | solution.py:112
  11.9 1.9 %collective-permute-done.2 = f32[64,128]{1,0:T(8,128)S(1)} collective-permute-done((f32[64,128]{1,0:T(8,128)S(1)}, f32[64,128]{1,0:T(8,128)S(1)}, u32[]{:S(2)}, u32[]{:S(2)}) %collective-permute-start.2) | collective-permute-done | bytes 32800 | tf_op jit(solution)/shard_map/ppermute | solution.py:112
  13.8 2.1 %collective-permute-start.3 = (f32[64,128]{1,0:T(8,128)S(1)}, f32[64,128]{1,0:T(8,128)S(1)}, u32[]{:S(2)}, u32[]{:S(2)}) collective-permute-start(f32[64,128]{1,0:T(8,128)S(1)} %add.17), channel_id=1, source_target_pairs={{0,1},{1,0},{2,3},{3,2},{4,5},{5,4},{6,7},{7,6},{8,9},{9,8},{10,11... | collective-permute-start | bytes 98312 | tf_op jit(solution)/shard_map/ppermute | solution.py:112
  15.8 1.9 %collective-permute-done.3 = f32[64,128]{1,0:T(8,128)S(1)} collective-permute-done((f32[64,128]{1,0:T(8,128)S(1)}, f32[64,128]{1,0:T(8,128)S(1)}, u32[]{:S(2)}, u32[]{:S(2)}) %collective-permute-start.3) | collective-permute-done | bytes 32800 | tf_op jit(solution)/shard_map/ppermute | solution.py:112
  17.7 3.0 %collective-permute-start.4 = (f32[64,128]{1,0:T(8,128)S(1)}, f32[64,128]{1,0:T(8,128)S(1)}, u32[]{:S(2)}, u32[]{:S(2)}) collective-permute-start(f32[64,128]{1,0:T(8,128)S(1)} %add.18), channel_id=1, source_target_pairs={{0,2},{1,3},{2,0},{3,1},{4,6},{5,7},{6,4},{7,5},{8,10},{9,11},{10,... | collective-permute-start | bytes 98312 | tf_op jit(solution)/shard_map/ppermute | solution.py:112
  20.8 1.9 %collective-permute-done.4 = f32[64,128]{1,0:T(8,128)S(1)} collective-permute-done((f32[64,128]{1,0:T(8,128)S(1)}, f32[64,128]{1,0:T(8,128)S(1)}, u32[]{:S(2)}, u32[]{:S(2)}) %collective-permute-start.4) | collective-permute-done | bytes 32800 | tf_op jit(solution)/shard_map/ppermute | solution.py:112
  22.7 0.0 copy-done
  22.7 8.6 %update.1 = (f32[32,8192]{1,0:T(8,128)}, f32[1,32]{1,0:T(1,128)}) custom-call(f32[64,128]{1,0:T(8,128)S(1)} %add.19.sums_ref, f32[1,32]{1,0:T(1,128)S(1)} %bitcast.2, f32[64,8192]{1,0:T(8,128)} %snap_ref.3, f32[32,8192]{1,0:T(8,128)} %basis_ref.3), custom_call_target="tpu_custom_call" | custom-call | tf_op jit(solution)/shard_map/update/pallas_call | solution.py:249
  (5 shorter events, 0.0 us)
Async XLA Ops:
  0.6 22.0 %copy-start = (f32[32]{0:T(128)S(1)}, f32[32]{0:T(128)}, u32[]{:S(2)}) copy-start(f32[32]{0:T(128)} %param.4) | copy-start | bytes 388
  3.7 1.4 %collective-permute-start = (f32[64,128]{1,0:T(8,128)S(1)}, f32[64,128]{1,0:T(8,128)S(1)}, u32[]{:S(2)}, u32[]{:S(2)}) collective-permute-start(f32[64,128]{1,0:T(8,128)S(1)} %gram.1), channel_id=1, source_target_pairs={{0,16},{16,0},{1,17},{17,1},{2,18},{18,2},{3,19},{19,3},{4,20},{20... | collective-permute-start | bytes 98312 | tf_op jit(solution)/shard_map/ppermute | solution.py:112
  5.1 4.7 %collective-permute-start.1 = (f32[64,128]{1,0:T(8,128)S(1)}, f32[64,128]{1,0:T(8,128)S(1)}, u32[]{:S(2)}, u32[]{:S(2)}) collective-permute-start(f32[64,128]{1,0:T(8,128)S(1)} %add.15), channel_id=1, source_target_pairs={{0,4},{4,0},{8,12},{12,8},{1,5},{5,1},{9,13},{13,9},{2,6},{6,2},{1... | collective-permute-start | bytes 98312 | tf_op jit(solution)/shard_map/ppermute | solution.py:112
  9.8 3.9 %collective-permute-start.2 = (f32[64,128]{1,0:T(8,128)S(1)}, f32[64,128]{1,0:T(8,128)S(1)}, u32[]{:S(2)}, u32[]{:S(2)}) collective-permute-start(f32[64,128]{1,0:T(8,128)S(1)} %add.16), channel_id=1, source_target_pairs={{0,8},{4,12},{8,0},{12,4},{1,9},{5,13},{9,1},{13,5},{2,10},{6,14},... | collective-permute-start | bytes 98312 | tf_op jit(solution)/shard_map/ppermute | solution.py:112
  13.8 4.0 %collective-permute-start.3 = (f32[64,128]{1,0:T(8,128)S(1)}, f32[64,128]{1,0:T(8,128)S(1)}, u32[]{:S(2)}, u32[]{:S(2)}) collective-permute-start(f32[64,128]{1,0:T(8,128)S(1)} %add.17), channel_id=1, source_target_pairs={{0,1},{1,0},{2,3},{3,2},{4,5},{5,4},{6,7},{7,6},{8,9},{9,8},{10,11... | collective-permute-start | bytes 98312 | tf_op jit(solution)/shard_map/ppermute | solution.py:112
  17.7 4.9 %collective-permute-start.4 = (f32[64,128]{1,0:T(8,128)S(1)}, f32[64,128]{1,0:T(8,128)S(1)}, u32[]{:S(2)}, u32[]{:S(2)}) collective-permute-start(f32[64,128]{1,0:T(8,128)S(1)} %add.18), channel_id=1, source_target_pairs={{0,2},{1,3},{2,0},{3,1},{4,6},{5,7},{6,4},{7,5},{8,10},{9,11},{10,... | collective-permute-start | bytes 98312 | tf_op jit(solution)/shard_map/ppermute | solution.py:112

commit v6 on v5

--- a/solution.py
+++ b/solution.py
@@ -79,8 +79,15 @@
     sent = out_ref.shape[1]
     rows = (total[:count] + total[count:]) * scale
     rows = rows[:, :count] + rows[:, count:]
-    corr = jnp.concatenate([rows[new:, new:], jnp.zeros((new - modes, modes), jnp.float32)], axis=0)
-    out_ref[...] = jnp.concatenate([rows[:new], corr], axis=1)
+    part = modes // 2
+    middle, last = rows[modes : modes + part], rows[modes + part : new]
+    out_ref[...] = jnp.concatenate(
+        [
+            jnp.concatenate([rows[:modes], rows[new:, new:]], axis=1),
+            jnp.concatenate([middle[:, modes:new], last[:, modes:new], middle[:, new:], last[:, new:]], axis=1),
+        ],
+        axis=0,
+    )
 
 
 def gram(snapshots, basis, total):
@@ -90,7 +97,7 @@
     count = new + modes
     return pl.pallas_call(
         functools.partial(gram_kernel, 1.0 / total, width),
-        out_shape=jax.ShapeDtypeStruct((new, count + modes), jnp.float32),
+        out_shape=jax.ShapeDtypeStruct((modes + modes // 2, count + modes), jnp.float32),
         in_specs=[pl.BlockSpec(memory_space=pltpu.HBM), pl.BlockSpec(memory_space=pltpu.HBM)],
         out_specs=pl.BlockSpec(memory_space=pltpu.VMEM),
         scratch_shapes=[
@@ -166,7 +173,12 @@
         load.start()
 
     half = sums_ref.shape[1]
-    top = sums_ref[...]
+    upper = sums_ref[:modes]
+    lower = sums_ref[modes:]
+    cross = upper[:, modes:new]
+    last = jnp.concatenate([lower[:, :modes], lower[:, modes:new]], axis=0)
+    snap_gram = jnp.concatenate([upper[:, :new], jnp.concatenate([cross.T, last], axis=1)], axis=0)
+    snap_gram = jnp.concatenate([snap_gram, jnp.zeros((new, half - new), jnp.float32)], axis=1)
     lane = lax.broadcasted_iota(jnp.int32, (modes, half), 1)
     line = lax.broadcasted_iota(jnp.int32, (modes, half), 0)
     wide = lax.broadcasted_iota(jnp.int32, (new, half), 1)
@@ -180,16 +192,20 @@
         under = half - place - x.shape[0]
         return jnp.concatenate(above + [x] + ([jnp.zeros((under, x.shape[1]), x.dtype)] if under else []), axis=0)
 
-    corr = jnp.where(lane >= count, top[:modes], 0.0)
+    corr = jnp.where(lane >= count, upper, 0.0)
     same = jnp.where(lane == count + line, 1.0, 0.0)
     twice = 2.0 * same - corr
-    pair = dot(jnp.where(wide < count, top, 0.0), at(new, jnp.concatenate([twice, same], axis=1)))
+    sent = jnp.concatenate([upper, lower, lower], axis=0)
+    late = lax.broadcasted_iota(jnp.int32, (new, half), 0) >= modes + modes // 2
+    sent = jnp.where((wide >= new) & ((wide >= count) == late), sent, 0.0)
+    both = jnp.concatenate([twice, same], axis=1)
+    pair = dot(sent, jnp.concatenate([jnp.zeros((new, 2 * half), jnp.float32), both, both], axis=0))
     joined_t, first_t = pair[:, :half], pair[:, half:]
     joined = dot(twice, at(0, first_t), NT)
     joined_at = dot(first_t, at(new, twice), NT)
     rest = first_t - dot(joined_t, at(count, corr))
     residual = (
-        jnp.where(wide < new, top, 0.0) - dot(joined_t, at(0, first_t), NT) - dot(rest, at(0, joined_t), NT)
+        snap_gram - dot(joined_t, at(0, first_t), NT) - dot(rest, at(0, joined_t), NT)
     )
     corner = jnp.where(lane == new + line, sigma * sigma, 0.0) + dot(joined, at(new, joined), NT)
     bend = dot(joined, at(0, residual))
@@ -244,7 +260,7 @@
     new, columns = snapshots.shape
     modes = basis.shape[0]
     count = new + modes
-    width = blocks_of(columns, 2048)
+    width = blocks_of(columns, 1024)
     half = count + modes
     return pl.pallas_call(
         functools.partial(update_kernel, width),

time: 31.4 us -> 31.1 us (level)
  waiting for transfers between devices: 8.43 us -> 8.06 us
    ppermute x5, waiting for transfers between devices: 8.43 us -> 8.06 us  [all_sum(): x = x + lax.ppermute(x, axis, [(i, i ^ bit) for i in range(size)])]
where the time goes in v6:
time: 31.1 us; the launch traced here: 30.9 us
  Pallas kernels  11.6 us (37%)
  starting transfers between devices  10.5 us (34%)
  waiting for transfers between devices  8.06 us (26%)
  between operations  0.66 us (2%)
    ppermute x5, starting transfers between devices, all_sum(): x = x + lax.ppermute(x, axis, [(i, i ^ bit) for i in range(size)])  10.5 us
    pallas_call x1, Pallas kernels, update(): pl.pallas_call(functools.partial(update_kernel, width), out_shape=(jax.Sh...  8.6 us
    ppermute x5, waiting for transfers between devices, all_sum(): x = x + lax.ppermute(x, axis, [(i, i ^ bit) for i in range(size)])  8.06 us
    pallas_call x1, Pallas kernels, gram(): pl.pallas_call(functools.partial(gram_kernel, 1.0 / total, width), out_sh...  3.01 us
  transfers between devices with their start and end apart: 5, of which 5 were waited for; matrix products, arithmetic and copies ran while one was open for 0% of the time, Pallas kernels for 0%

profile of v6, /device:TPU:0, one launch (start us, length us, event | category | flops | bytes accessed | tf_op | source)
XLA Modules:
  0.0 30.9 jit_solution(6927675667133342762)
XLA Ops:
  0.6 0.0 copy-start
  0.6 3.0 %gram.1 = f32[48,128]{1,0:T(8,128)S(1)} custom-call(f32[64,8192]{1,0:T(8,128)} %snap_ref.3, f32[32,8192]{1,0:T(8,128)} %basis_ref.3), custom_call_target="tpu_custom_call" | custom-call | tf_op jit(solution)/shard_map/gram/pallas_call | solution.py:98
  3.7 0.6 %collective-permute-start = (f32[48,128]{1,0:T(8,128)S(1)}, f32[48,128]{1,0:T(8,128)S(1)}, u32[]{:S(2)}, u32[]{:S(2)}) collective-permute-start(f32[48,128]{1,0:T(8,128)S(1)} %gram.1), channel_id=1, source_target_pairs={{0,16},{16,0},{1,17},{17,1},{2,18},{18,2},{3,19},{19,3},{4,20},{20... | collective-permute-start | bytes 73736 | tf_op jit(solution)/shard_map/ppermute | solution.py:119
  4.2 0.8 %collective-permute-done = f32[48,128]{1,0:T(8,128)S(1)} collective-permute-done((f32[48,128]{1,0:T(8,128)S(1)}, f32[48,128]{1,0:T(8,128)S(1)}, u32[]{:S(2)}, u32[]{:S(2)}) %collective-permute-start) | collective-permute-done | bytes 24608 | tf_op jit(solution)/shard_map/ppermute | solution.py:119
  5.1 2.8 %collective-permute-start.1 = (f32[48,128]{1,0:T(8,128)S(1)}, f32[48,128]{1,0:T(8,128)S(1)}, u32[]{:S(2)}, u32[]{:S(2)}) collective-permute-start(f32[48,128]{1,0:T(8,128)S(1)} %add.15), channel_id=1, source_target_pairs={{0,4},{4,0},{8,12},{12,8},{1,5},{5,1},{9,13},{13,9},{2,6},{6,2},{1... | collective-permute-start | bytes 73736 | tf_op jit(solution)/shard_map/ppermute | solution.py:119
  7.9 1.8 %collective-permute-done.1 = f32[48,128]{1,0:T(8,128)S(1)} collective-permute-done((f32[48,128]{1,0:T(8,128)S(1)}, f32[48,128]{1,0:T(8,128)S(1)}, u32[]{:S(2)}, u32[]{:S(2)}) %collective-permute-start.1) | collective-permute-done | bytes 24608 | tf_op jit(solution)/shard_map/ppermute | solution.py:119
  9.7 2.1 %collective-permute-start.2 = (f32[48,128]{1,0:T(8,128)S(1)}, f32[48,128]{1,0:T(8,128)S(1)}, u32[]{:S(2)}, u32[]{:S(2)}) collective-permute-start(f32[48,128]{1,0:T(8,128)S(1)} %add.16), channel_id=1, source_target_pairs={{0,8},{4,12},{8,0},{12,4},{1,9},{5,13},{9,1},{13,5},{2,10},{6,14},... | collective-permute-start | bytes 73736 | tf_op jit(solution)/shard_map/ppermute | solution.py:119
  11.8 1.8 %collective-permute-done.2 = f32[48,128]{1,0:T(8,128)S(1)} collective-permute-done((f32[48,128]{1,0:T(8,128)S(1)}, f32[48,128]{1,0:T(8,128)S(1)}, u32[]{:S(2)}, u32[]{:S(2)}) %collective-permute-start.2) | collective-permute-done | bytes 24608 | tf_op jit(solution)/shard_map/ppermute | solution.py:119
  13.6 2.1 %collective-permute-start.3 = (f32[48,128]{1,0:T(8,128)S(1)}, f32[48,128]{1,0:T(8,128)S(1)}, u32[]{:S(2)}, u32[]{:S(2)}) collective-permute-start(f32[48,128]{1,0:T(8,128)S(1)} %add.17), channel_id=1, source_target_pairs={{0,1},{1,0},{2,3},{3,2},{4,5},{5,4},{6,7},{7,6},{8,9},{9,8},{10,11... | collective-permute-start | bytes 73736 | tf_op jit(solution)/shard_map/ppermute | solution.py:119
  15.6 1.8 %collective-permute-done.3 = f32[48,128]{1,0:T(8,128)S(1)} collective-permute-done((f32[48,128]{1,0:T(8,128)S(1)}, f32[48,128]{1,0:T(8,128)S(1)}, u32[]{:S(2)}, u32[]{:S(2)}) %collective-permute-start.3) | collective-permute-done | bytes 24608 | tf_op jit(solution)/shard_map/ppermute | solution.py:119
  17.4 3.0 %collective-permute-start.4 = (f32[48,128]{1,0:T(8,128)S(1)}, f32[48,128]{1,0:T(8,128)S(1)}, u32[]{:S(2)}, u32[]{:S(2)}) collective-permute-start(f32[48,128]{1,0:T(8,128)S(1)} %add.18), channel_id=1, source_target_pairs={{0,2},{1,3},{2,0},{3,1},{4,6},{5,7},{6,4},{7,5},{8,10},{9,11},{10,... | collective-permute-start | bytes 73736 | tf_op jit(solution)/shard_map/ppermute | solution.py:119
  20.5 1.8 %collective-permute-done.4 = f32[48,128]{1,0:T(8,128)S(1)} collective-permute-done((f32[48,128]{1,0:T(8,128)S(1)}, f32[48,128]{1,0:T(8,128)S(1)}, u32[]{:S(2)}, u32[]{:S(2)}) %collective-permute-start.4) | collective-permute-done | bytes 24608 | tf_op jit(solution)/shard_map/ppermute | solution.py:119
  22.3 0.0 copy-done
  22.3 8.6 %update.1 = (f32[32,8192]{1,0:T(8,128)}, f32[1,32]{1,0:T(1,128)}) custom-call(f32[48,128]{1,0:T(8,128)S(1)} %add.19.sums_ref, f32[1,32]{1,0:T(1,128)S(1)} %bitcast.2, f32[64,8192]{1,0:T(8,128)} %snap_ref.3, f32[32,8192]{1,0:T(8,128)} %basis_ref.3), custom_call_target="tpu_custom_call" | custom-call | tf_op jit(solution)/shard_map/update/pallas_call | solution.py:265
  (5 shorter events, 0.0 us)
Async XLA Ops:
  0.6 21.7 %copy-start = (f32[32]{0:T(128)S(1)}, f32[32]{0:T(128)}, u32[]{:S(2)}) copy-start(f32[32]{0:T(128)} %param.4) | copy-start | bytes 388
  3.7 1.4 %collective-permute-start = (f32[48,128]{1,0:T(8,128)S(1)}, f32[48,128]{1,0:T(8,128)S(1)}, u32[]{:S(2)}, u32[]{:S(2)}) collective-permute-start(f32[48,128]{1,0:T(8,128)S(1)} %gram.1), channel_id=1, source_target_pairs={{0,16},{16,0},{1,17},{17,1},{2,18},{18,2},{3,19},{19,3},{4,20},{20... | collective-permute-start | bytes 73736 | tf_op jit(solution)/shard_map/ppermute | solution.py:119
  5.1 4.6 %collective-permute-start.1 = (f32[48,128]{1,0:T(8,128)S(1)}, f32[48,128]{1,0:T(8,128)S(1)}, u32[]{:S(2)}, u32[]{:S(2)}) collective-permute-start(f32[48,128]{1,0:T(8,128)S(1)} %add.15), channel_id=1, source_target_pairs={{0,4},{4,0},{8,12},{12,8},{1,5},{5,1},{9,13},{13,9},{2,6},{6,2},{1... | collective-permute-start | bytes 73736 | tf_op jit(solution)/shard_map/ppermute | solution.py:119
  9.7 3.9 %collective-permute-start.2 = (f32[48,128]{1,0:T(8,128)S(1)}, f32[48,128]{1,0:T(8,128)S(1)}, u32[]{:S(2)}, u32[]{:S(2)}) collective-permute-start(f32[48,128]{1,0:T(8,128)S(1)} %add.16), channel_id=1, source_target_pairs={{0,8},{4,12},{8,0},{12,4},{1,9},{5,13},{9,1},{13,5},{2,10},{6,14},... | collective-permute-start | bytes 73736 | tf_op jit(solution)/shard_map/ppermute | solution.py:119
  13.6 3.9 %collective-permute-start.3 = (f32[48,128]{1,0:T(8,128)S(1)}, f32[48,128]{1,0:T(8,128)S(1)}, u32[]{:S(2)}, u32[]{:S(2)}) collective-permute-start(f32[48,128]{1,0:T(8,128)S(1)} %add.17), channel_id=1, source_target_pairs={{0,1},{1,0},{2,3},{3,2},{4,5},{5,4},{6,7},{7,6},{8,9},{9,8},{10,11... | collective-permute-start | bytes 73736 | tf_op jit(solution)/shard_map/ppermute | solution.py:119
  17.4 4.8 %collective-permute-start.4 = (f32[48,128]{1,0:T(8,128)S(1)}, f32[48,128]{1,0:T(8,128)S(1)}, u32[]{:S(2)}, u32[]{:S(2)}) collective-permute-start(f32[48,128]{1,0:T(8,128)S(1)} %add.18), channel_id=1, source_target_pairs={{0,2},{1,3},{2,0},{3,1},{4,6},{5,7},{6,4},{7,5},{8,10},{9,11},{10,... | collective-permute-start | bytes 73736 | tf_op jit(solution)/shard_map/ppermute | solution.py:119

commit v7 on v6

--- a/solution.py
+++ b/solution.py
@@ -123,25 +123,27 @@
 
 def normalize(square, parts):
     n, lanes = square.shape[0], parts[0].shape[1]
-    groups = n // 8
+    groups, late = n // 8, min(n, 16)
     row = lax.broadcasted_iota(jnp.int32, (8, lanes), 0)
     parts = [[p[8 * q : 8 * q + 8] for q in range(groups)] for p in parts]
-    spread = [
-        [
-            jnp.broadcast_to(square[8 * q : 8 * q + 8, l : l + 1], (8, lanes)) if q >= l // 8 else None
-            for q in range(groups)
-        ]
-        for l in range(n)
-    ]
+    square = [square[8 * q : 8 * q + 8] for q in range(groups)]
+
+    def spread_of(l):
+        return [jnp.broadcast_to(square[q][:, l : l + 1], (8, lanes)) if q >= l // 8 else None for q in range(groups)]
+
+    spread = [spread_of(l) if l < late else None for l in range(n)]
     pivots = [jnp.ones((8, lanes), jnp.float32) for _ in range(groups)]
     for k in range(n):
         own, r = k // 8, k % 8
+        if k == 8:
+            for l in range(late, n):
+                spread[l] = spread_of(l)
         column = spread[k]
         pivot = jnp.broadcast_to(column[own][r : r + 1], (8, lanes))
-        pivots[own] = jnp.where(row == r, pivot, pivots[own])
+        pivots[own] = jnp.where(row == r, column[own], pivots[own])
         inverse = 1.0 / pivot
         scaled = [None if c is None else c * inverse for c in column]
-        for l in range(k + 1, n):
+        for l in range(k + 1, n if k >= 8 else late):
             entry = jnp.broadcast_to(column[l // 8][l % 8 : l % 8 + 1], (8, lanes))
             for q in range(l // 8, groups):
                 if l == k + 1:
@@ -149,6 +151,10 @@
                 else:
                     spread[l][q] = spread[l][q] - scaled[q] * entry
         below = jnp.where(row > r, scaled[own], 0.0)
+        if k < 8:
+            line = jnp.broadcast_to(square[0][r : r + 1], (8, n))
+            for q in [0] * (r < 7) + list(range(late // 8, groups)):
+                square[q] = square[q] - (below if q == 0 else scaled[q])[:, :n] * line
         for p in parts:
             line = jnp.broadcast_to(p[own][r : r + 1], (8, lanes))
             if r < 7:

time: 31.1 us -> 30.5 us (0.981)
  Pallas kernels: 11.6 us -> 11.1 us
    pallas_call x1, Pallas kernels: 8.6 us -> 8.08 us  [update(): pl.pallas_call(functools.partial(update_kernel, width), out_shape=(jax.Sh...]
where the time goes in v7:
time: 30.5 us; the launch traced here: 30.4 us
  Pallas kernels  11.1 us (36%)
  starting transfers between devices  10.5 us (34%)
  waiting for transfers between devices  8.06 us (26%)
  between operations  0.66 us (2%)
    ppermute x5, starting transfers between devices, all_sum(): x = x + lax.ppermute(x, axis, [(i, i ^ bit) for i in range(size)])  10.5 us
    pallas_call x1, Pallas kernels, update(): pl.pallas_call(functools.partial(update_kernel, width), out_shape=(jax.Sh...  8.08 us
    ppermute x5, waiting for transfers between devices, all_sum(): x = x + lax.ppermute(x, axis, [(i, i ^ bit) for i in range(size)])  8.06 us
    pallas_call x1, Pallas kernels, gram(): pl.pallas_call(functools.partial(gram_kernel, 1.0 / total, width), out_sh...  3.01 us
  transfers between devices with their start and end apart: 5, of which 5 were waited for; matrix products, arithmetic and copies ran while one was open for 0% of the time, Pallas kernels for 0%

profile of v7, /device:TPU:0, one launch (start us, length us, event | category | flops | bytes accessed | tf_op | source)
XLA Modules:
  0.0 30.4 jit_solution(4772794571525854221)
XLA Ops:
  0.6 0.0 copy-start
  0.6 3.0 %gram.1 = f32[48,128]{1,0:T(8,128)S(1)} custom-call(f32[64,8192]{1,0:T(8,128)} %snap_ref.3, f32[32,8192]{1,0:T(8,128)} %basis_ref.3), custom_call_target="tpu_custom_call" | custom-call | tf_op jit(solution)/shard_map/gram/pallas_call | solution.py:98
  3.7 0.6 %collective-permute-start = (f32[48,128]{1,0:T(8,128)S(1)}, f32[48,128]{1,0:T(8,128)S(1)}, u32[]{:S(2)}, u32[]{:S(2)}) collective-permute-start(f32[48,128]{1,0:T(8,128)S(1)} %gram.1), channel_id=1, source_target_pairs={{0,16},{16,0},{1,17},{17,1},{2,18},{18,2},{3,19},{19,3},{4,20},{20... | collective-permute-start | bytes 73736 | tf_op jit(solution)/shard_map/ppermute | solution.py:119
  4.2 0.8 %collective-permute-done = f32[48,128]{1,0:T(8,128)S(1)} collective-permute-done((f32[48,128]{1,0:T(8,128)S(1)}, f32[48,128]{1,0:T(8,128)S(1)}, u32[]{:S(2)}, u32[]{:S(2)}) %collective-permute-start) | collective-permute-done | bytes 24608 | tf_op jit(solution)/shard_map/ppermute | solution.py:119
  5.1 2.8 %collective-permute-start.1 = (f32[48,128]{1,0:T(8,128)S(1)}, f32[48,128]{1,0:T(8,128)S(1)}, u32[]{:S(2)}, u32[]{:S(2)}) collective-permute-start(f32[48,128]{1,0:T(8,128)S(1)} %add.15), channel_id=1, source_target_pairs={{0,4},{4,0},{8,12},{12,8},{1,5},{5,1},{9,13},{13,9},{2,6},{6,2},{1... | collective-permute-start | bytes 73736 | tf_op jit(solution)/shard_map/ppermute | solution.py:119
  7.9 1.8 %collective-permute-done.1 = f32[48,128]{1,0:T(8,128)S(1)} collective-permute-done((f32[48,128]{1,0:T(8,128)S(1)}, f32[48,128]{1,0:T(8,128)S(1)}, u32[]{:S(2)}, u32[]{:S(2)}) %collective-permute-start.1) | collective-permute-done | bytes 24608 | tf_op jit(solution)/shard_map/ppermute | solution.py:119
  9.7 2.1 %collective-permute-start.2 = (f32[48,128]{1,0:T(8,128)S(1)}, f32[48,128]{1,0:T(8,128)S(1)}, u32[]{:S(2)}, u32[]{:S(2)}) collective-permute-start(f32[48,128]{1,0:T(8,128)S(1)} %add.16), channel_id=1, source_target_pairs={{0,8},{4,12},{8,0},{12,4},{1,9},{5,13},{9,1},{13,5},{2,10},{6,14},... | collective-permute-start | bytes 73736 | tf_op jit(solution)/shard_map/ppermute | solution.py:119
  11.8 1.8 %collective-permute-done.2 = f32[48,128]{1,0:T(8,128)S(1)} collective-permute-done((f32[48,128]{1,0:T(8,128)S(1)}, f32[48,128]{1,0:T(8,128)S(1)}, u32[]{:S(2)}, u32[]{:S(2)}) %collective-permute-start.2) | collective-permute-done | bytes 24608 | tf_op jit(solution)/shard_map/ppermute | solution.py:119
  13.6 2.1 %collective-permute-start.3 = (f32[48,128]{1,0:T(8,128)S(1)}, f32[48,128]{1,0:T(8,128)S(1)}, u32[]{:S(2)}, u32[]{:S(2)}) collective-permute-start(f32[48,128]{1,0:T(8,128)S(1)} %add.17), channel_id=1, source_target_pairs={{0,1},{1,0},{2,3},{3,2},{4,5},{5,4},{6,7},{7,6},{8,9},{9,8},{10,11... | collective-permute-start | bytes 73736 | tf_op jit(solution)/shard_map/ppermute | solution.py:119
  15.6 1.8 %collective-permute-done.3 = f32[48,128]{1,0:T(8,128)S(1)} collective-permute-done((f32[48,128]{1,0:T(8,128)S(1)}, f32[48,128]{1,0:T(8,128)S(1)}, u32[]{:S(2)}, u32[]{:S(2)}) %collective-permute-start.3) | collective-permute-done | bytes 24608 | tf_op jit(solution)/shard_map/ppermute | solution.py:119
  17.4 3.0 %collective-permute-start.4 = (f32[48,128]{1,0:T(8,128)S(1)}, f32[48,128]{1,0:T(8,128)S(1)}, u32[]{:S(2)}, u32[]{:S(2)}) collective-permute-start(f32[48,128]{1,0:T(8,128)S(1)} %add.18), channel_id=1, source_target_pairs={{0,2},{1,3},{2,0},{3,1},{4,6},{5,7},{6,4},{7,5},{8,10},{9,11},{10,... | collective-permute-start | bytes 73736 | tf_op jit(solution)/shard_map/ppermute | solution.py:119
  20.5 1.8 %collective-permute-done.4 = f32[48,128]{1,0:T(8,128)S(1)} collective-permute-done((f32[48,128]{1,0:T(8,128)S(1)}, f32[48,128]{1,0:T(8,128)S(1)}, u32[]{:S(2)}, u32[]{:S(2)}) %collective-permute-start.4) | collective-permute-done | bytes 24608 | tf_op jit(solution)/shard_map/ppermute | solution.py:119
  22.3 0.0 copy-done
  22.3 8.1 %update.1 = (f32[32,8192]{1,0:T(8,128)}, f32[1,32]{1,0:T(1,128)}) custom-call(f32[48,128]{1,0:T(8,128)S(1)} %add.19.sums_ref, f32[1,32]{1,0:T(1,128)S(1)} %bitcast.2, f32[64,8192]{1,0:T(8,128)} %snap_ref.3, f32[32,8192]{1,0:T(8,128)} %basis_ref.3), custom_call_target="tpu_custom_call" | custom-call | tf_op jit(solution)/shard_map/update/pallas_call | solution.py:271
  (5 shorter events, 0.0 us)
Async XLA Ops:
  0.6 21.7 %copy-start = (f32[32]{0:T(128)S(1)}, f32[32]{0:T(128)}, u32[]{:S(2)}) copy-start(f32[32]{0:T(128)} %param.4) | copy-start | bytes 388
  3.7 1.4 %collective-permute-start = (f32[48,128]{1,0:T(8,128)S(1)}, f32[48,128]{1,0:T(8,128)S(1)}, u32[]{:S(2)}, u32[]{:S(2)}) collective-permute-start(f32[48,128]{1,0:T(8,128)S(1)} %gram.1), channel_id=1, source_target_pairs={{0,16},{16,0},{1,17},{17,1},{2,18},{18,2},{3,19},{19,3},{4,20},{20... | collective-permute-start | bytes 73736 | tf_op jit(solution)/shard_map/ppermute | solution.py:119
  5.1 4.6 %collective-permute-start.1 = (f32[48,128]{1,0:T(8,128)S(1)}, f32[48,128]{1,0:T(8,128)S(1)}, u32[]{:S(2)}, u32[]{:S(2)}) collective-permute-start(f32[48,128]{1,0:T(8,128)S(1)} %add.15), channel_id=1, source_target_pairs={{0,4},{4,0},{8,12},{12,8},{1,5},{5,1},{9,13},{13,9},{2,6},{6,2},{1... | collective-permute-start | bytes 73736 | tf_op jit(solution)/shard_map/ppermute | solution.py:119
  9.7 3.9 %collective-permute-start.2 = (f32[48,128]{1,0:T(8,128)S(1)}, f32[48,128]{1,0:T(8,128)S(1)}, u32[]{:S(2)}, u32[]{:S(2)}) collective-permute-start(f32[48,128]{1,0:T(8,128)S(1)} %add.16), channel_id=1, source_target_pairs={{0,8},{4,12},{8,0},{12,4},{1,9},{5,13},{9,1},{13,5},{2,10},{6,14},... | collective-permute-start | bytes 73736 | tf_op jit(solution)/shard_map/ppermute | solution.py:119
  13.6 3.9 %collective-permute-start.3 = (f32[48,128]{1,0:T(8,128)S(1)}, f32[48,128]{1,0:T(8,128)S(1)}, u32[]{:S(2)}, u32[]{:S(2)}) collective-permute-start(f32[48,128]{1,0:T(8,128)S(1)} %add.17), channel_id=1, source_target_pairs={{0,1},{1,0},{2,3},{3,2},{4,5},{5,4},{6,7},{7,6},{8,9},{9,8},{10,11... | collective-permute-start | bytes 73736 | tf_op jit(solution)/shard_map/ppermute | solution.py:119
  17.4 4.8 %collective-permute-start.4 = (f32[48,128]{1,0:T(8,128)S(1)}, f32[48,128]{1,0:T(8,128)S(1)}, u32[]{:S(2)}, u32[]{:S(2)}) collective-permute-start(f32[48,128]{1,0:T(8,128)S(1)} %add.18), channel_id=1, source_target_pairs={{0,2},{1,3},{2,0},{3,1},{4,6},{5,7},{6,4},{7,5},{8,10},{9,11},{10,... | collective-permute-start | bytes 73736 | tf_op jit(solution)/shard_map/ppermute | solution.py:119

commit v8 on v6

--- a/solution.py
+++ b/solution.py
@@ -8,6 +8,7 @@
 from jax.sharding import PartitionSpec as P
 
 ITERS = 4
+LEAD = 8
 GRAM_WIDTH = 4096
 GRANT = 24 * 1024 * 1024
 AXES = ("gx", "gy", "gz")
@@ -121,27 +122,36 @@
     return x
 
 
-def normalize(square, parts):
-    n, lanes = square.shape[0], parts[0].shape[1]
+def normalize(left, right, others):
+    n, lanes = left.shape
     groups = n // 8
     row = lax.broadcasted_iota(jnp.int32, (8, lanes), 0)
-    parts = [[p[8 * q : 8 * q + 8] for q in range(groups)] for p in parts]
-    spread = [
-        [
-            jnp.broadcast_to(square[8 * q : 8 * q + 8, l : l + 1], (8, lanes)) if q >= l // 8 else None
+    parts = [[p[8 * q : 8 * q + 8] for q in range(groups)] for p in (left, *others)]
+
+    def start(l):
+        return max(0, l // 8 * 8 - LEAD)
+
+    def column_of(l):
+        line = jnp.broadcast_to(right[l : l + 1], (8, lanes))
+        return [
+            jnp.broadcast_to(jnp.sum(parts[0][q] * line, axis=1, keepdims=True), (8, lanes)) if q >= l // 8 else None
             for q in range(groups)
         ]
-        for l in range(n)
-    ]
+
+    spread = [None] * n
     pivots = [jnp.ones((8, lanes), jnp.float32) for _ in range(groups)]
     for k in range(n):
         own, r = k // 8, k % 8
+        for l in range(k, n):
+            if start(l) == k:
+                spread[l] = column_of(l)
         column = spread[k]
-        pivot = jnp.broadcast_to(column[own][r : r + 1], (8, lanes))
-        pivots[own] = jnp.where(row == r, pivot, pivots[own])
-        inverse = 1.0 / pivot
+        pivots[own] = jnp.where(row == r, column[own], pivots[own])
+        inverse = 1.0 / jnp.broadcast_to(column[own][r : r + 1], (8, lanes))
         scaled = [None if c is None else c * inverse for c in column]
         for l in range(k + 1, n):
+            if start(l) > k:
+                continue
             entry = jnp.broadcast_to(column[l // 8][l % 8 : l % 8 + 1], (8, lanes))
             for q in range(l // 8, groups):
                 if l == k + 1:
@@ -220,12 +230,9 @@
     step_ref[...] = as_right(step, 0)
 
     def iterate(_, parts):
-        left, right = normalize(dot(*parts, NT), parts)
-        right = as_left(right)
-        after = product_of(right, step_ref[...])
-        high, middle, last = right[:, :half], right[:, half : 2 * half], right[:, 3 * half : 4 * half]
-        square = product_of(as_left(left), jnp.concatenate([high, high, middle, high, middle, last], axis=1), NT)
-        left, *after = normalize(square, [left, after[:, :half], after[:, half:]])
+        left, right = normalize(*parts, [parts[1]])
+        after = product_of(as_left(right), step_ref[...])
+        left, *after = normalize(left, right, [after[:, :half], after[:, half:]])
         frame_ref[...] = left
         return tuple(after)
 

time: 31.1 us -> 29.1 us (0.936)
  Pallas kernels: 11.6 us -> 9.7 us
    pallas_call x1, Pallas kernels: 8.6 us -> 6.69 us  [update(): pl.pallas_call(functools.partial(update_kernel, width), out_shape=(jax.Sh...]
where the time goes in v8:
time: 29.1 us; the launch traced here: 29 us
  starting transfers between devices  10.5 us (36%)
  Pallas kernels  9.7 us (33%)
  waiting for transfers between devices  8.06 us (28%)
  between operations  0.66 us (2%)
    ppermute x5, starting transfers between devices, all_sum(): x = x + lax.ppermute(x, axis, [(i, i ^ bit) for i in range(size)])  10.5 us
    ppermute x5, waiting for transfers between devices, all_sum(): x = x + lax.ppermute(x, axis, [(i, i ^ bit) for i in range(size)])  8.06 us
    pallas_call x1, Pallas kernels, update(): pl.pallas_call(functools.partial(update_kernel, width), out_shape=(jax.Sh...  6.69 us
    pallas_call x1, Pallas kernels, gram(): pl.pallas_call(functools.partial(gram_kernel, 1.0 / total, width), out_sh...  3.01 us
  transfers between devices with their start and end apart: 5, of which 5 were waited for; matrix products, arithmetic and copies ran while one was open for 0% of the time, Pallas kernels for 0%

profile of v8, /device:TPU:0, one launch (start us, length us, event | category | flops | bytes accessed | tf_op | source)
XLA Modules:
  0.0 29.0 jit_solution(15407914031412627384)
XLA Ops:
  0.6 0.0 copy-start
  0.6 3.0 %gram.1 = f32[48,128]{1,0:T(8,128)S(1)} custom-call(f32[64,8192]{1,0:T(8,128)} %snap_ref.3, f32[32,8192]{1,0:T(8,128)} %basis_ref.3), custom_call_target="tpu_custom_call" | custom-call | tf_op jit(solution)/shard_map/gram/pallas_call | solution.py:99
  3.7 0.6 %collective-permute-start = (f32[48,128]{1,0:T(8,128)S(1)}, f32[48,128]{1,0:T(8,128)S(1)}, u32[]{:S(2)}, u32[]{:S(2)}) collective-permute-start(f32[48,128]{1,0:T(8,128)S(1)} %gram.1), channel_id=1, source_target_pairs={{0,16},{16,0},{1,17},{17,1},{2,18},{18,2},{3,19},{19,3},{4,20},{20... | collective-permute-start | bytes 73736 | tf_op jit(solution)/shard_map/ppermute | solution.py:120
  4.2 0.8 %collective-permute-done = f32[48,128]{1,0:T(8,128)S(1)} collective-permute-done((f32[48,128]{1,0:T(8,128)S(1)}, f32[48,128]{1,0:T(8,128)S(1)}, u32[]{:S(2)}, u32[]{:S(2)}) %collective-permute-start) | collective-permute-done | bytes 24608 | tf_op jit(solution)/shard_map/ppermute | solution.py:120
  5.1 2.8 %collective-permute-start.1 = (f32[48,128]{1,0:T(8,128)S(1)}, f32[48,128]{1,0:T(8,128)S(1)}, u32[]{:S(2)}, u32[]{:S(2)}) collective-permute-start(f32[48,128]{1,0:T(8,128)S(1)} %add.15), channel_id=1, source_target_pairs={{0,4},{4,0},{8,12},{12,8},{1,5},{5,1},{9,13},{13,9},{2,6},{6,2},{1... | collective-permute-start | bytes 73736 | tf_op jit(solution)/shard_map/ppermute | solution.py:120
  7.9 1.8 %collective-permute-done.1 = f32[48,128]{1,0:T(8,128)S(1)} collective-permute-done((f32[48,128]{1,0:T(8,128)S(1)}, f32[48,128]{1,0:T(8,128)S(1)}, u32[]{:S(2)}, u32[]{:S(2)}) %collective-permute-start.1) | collective-permute-done | bytes 24608 | tf_op jit(solution)/shard_map/ppermute | solution.py:120
  9.7 2.1 %collective-permute-start.2 = (f32[48,128]{1,0:T(8,128)S(1)}, f32[48,128]{1,0:T(8,128)S(1)}, u32[]{:S(2)}, u32[]{:S(2)}) collective-permute-start(f32[48,128]{1,0:T(8,128)S(1)} %add.16), channel_id=1, source_target_pairs={{0,8},{4,12},{8,0},{12,4},{1,9},{5,13},{9,1},{13,5},{2,10},{6,14},... | collective-permute-start | bytes 73736 | tf_op jit(solution)/shard_map/ppermute | solution.py:120
  11.8 1.8 %collective-permute-done.2 = f32[48,128]{1,0:T(8,128)S(1)} collective-permute-done((f32[48,128]{1,0:T(8,128)S(1)}, f32[48,128]{1,0:T(8,128)S(1)}, u32[]{:S(2)}, u32[]{:S(2)}) %collective-permute-start.2) | collective-permute-done | bytes 24608 | tf_op jit(solution)/shard_map/ppermute | solution.py:120
  13.6 2.1 %collective-permute-start.3 = (f32[48,128]{1,0:T(8,128)S(1)}, f32[48,128]{1,0:T(8,128)S(1)}, u32[]{:S(2)}, u32[]{:S(2)}) collective-permute-start(f32[48,128]{1,0:T(8,128)S(1)} %add.17), channel_id=1, source_target_pairs={{0,1},{1,0},{2,3},{3,2},{4,5},{5,4},{6,7},{7,6},{8,9},{9,8},{10,11... | collective-permute-start | bytes 73736 | tf_op jit(solution)/shard_map/ppermute | solution.py:120
  15.6 1.8 %collective-permute-done.3 = f32[48,128]{1,0:T(8,128)S(1)} collective-permute-done((f32[48,128]{1,0:T(8,128)S(1)}, f32[48,128]{1,0:T(8,128)S(1)}, u32[]{:S(2)}, u32[]{:S(2)}) %collective-permute-start.3) | collective-permute-done | bytes 24608 | tf_op jit(solution)/shard_map/ppermute | solution.py:120
  17.4 3.0 %collective-permute-start.4 = (f32[48,128]{1,0:T(8,128)S(1)}, f32[48,128]{1,0:T(8,128)S(1)}, u32[]{:S(2)}, u32[]{:S(2)}) collective-permute-start(f32[48,128]{1,0:T(8,128)S(1)} %add.18), channel_id=1, source_target_pairs={{0,2},{1,3},{2,0},{3,1},{4,6},{5,7},{6,4},{7,5},{8,10},{9,11},{10,... | collective-permute-start | bytes 73736 | tf_op jit(solution)/shard_map/ppermute | solution.py:120
  20.5 1.8 %collective-permute-done.4 = f32[48,128]{1,0:T(8,128)S(1)} collective-permute-done((f32[48,128]{1,0:T(8,128)S(1)}, f32[48,128]{1,0:T(8,128)S(1)}, u32[]{:S(2)}, u32[]{:S(2)}) %collective-permute-start.4) | collective-permute-done | bytes 24608 | tf_op jit(solution)/shard_map/ppermute | solution.py:120
  22.3 0.0 copy-done
  22.3 6.7 %update.1 = (f32[32,8192]{1,0:T(8,128)}, f32[1,32]{1,0:T(1,128)}) custom-call(f32[48,128]{1,0:T(8,128)S(1)} %add.19.sums_ref, f32[1,32]{1,0:T(1,128)S(1)} %bitcast.2, f32[64,8192]{1,0:T(8,128)} %snap_ref.3, f32[32,8192]{1,0:T(8,128)} %basis_ref.3), custom_call_target="tpu_custom_call" | custom-call | tf_op jit(solution)/shard_map/update/pallas_call | solution.py:272
  (5 shorter events, 0.0 us)
Async XLA Ops:
  0.6 21.7 %copy-start = (f32[32]{0:T(128)S(1)}, f32[32]{0:T(128)}, u32[]{:S(2)}) copy-start(f32[32]{0:T(128)} %param.4) | copy-start | bytes 388
  3.7 1.4 %collective-permute-start = (f32[48,128]{1,0:T(8,128)S(1)}, f32[48,128]{1,0:T(8,128)S(1)}, u32[]{:S(2)}, u32[]{:S(2)}) collective-permute-start(f32[48,128]{1,0:T(8,128)S(1)} %gram.1), channel_id=1, source_target_pairs={{0,16},{16,0},{1,17},{17,1},{2,18},{18,2},{3,19},{19,3},{4,20},{20... | collective-permute-start | bytes 73736 | tf_op jit(solution)/shard_map/ppermute | solution.py:120
  5.1 4.6 %collective-permute-start.1 = (f32[48,128]{1,0:T(8,128)S(1)}, f32[48,128]{1,0:T(8,128)S(1)}, u32[]{:S(2)}, u32[]{:S(2)}) collective-permute-start(f32[48,128]{1,0:T(8,128)S(1)} %add.15), channel_id=1, source_target_pairs={{0,4},{4,0},{8,12},{12,8},{1,5},{5,1},{9,13},{13,9},{2,6},{6,2},{1... | collective-permute-start | bytes 73736 | tf_op jit(solution)/shard_map/ppermute | solution.py:120
  9.7 3.9 %collective-permute-start.2 = (f32[48,128]{1,0:T(8,128)S(1)}, f32[48,128]{1,0:T(8,128)S(1)}, u32[]{:S(2)}, u32[]{:S(2)}) collective-permute-start(f32[48,128]{1,0:T(8,128)S(1)} %add.16), channel_id=1, source_target_pairs={{0,8},{4,12},{8,0},{12,4},{1,9},{5,13},{9,1},{13,5},{2,10},{6,14},... | collective-permute-start | bytes 73736 | tf_op jit(solution)/shard_map/ppermute | solution.py:120
  13.6 3.9 %collective-permute-start.3 = (f32[48,128]{1,0:T(8,128)S(1)}, f32[48,128]{1,0:T(8,128)S(1)}, u32[]{:S(2)}, u32[]{:S(2)}) collective-permute-start(f32[48,128]{1,0:T(8,128)S(1)} %add.17), channel_id=1, source_target_pairs={{0,1},{1,0},{2,3},{3,2},{4,5},{5,4},{6,7},{7,6},{8,9},{9,8},{10,11... | collective-permute-start | bytes 73736 | tf_op jit(solution)/shard_map/ppermute | solution.py:120
  17.4 4.8 %collective-permute-start.4 = (f32[48,128]{1,0:T(8,128)S(1)}, f32[48,128]{1,0:T(8,128)S(1)}, u32[]{:S(2)}, u32[]{:S(2)}) collective-permute-start(f32[48,128]{1,0:T(8,128)S(1)} %add.18), channel_id=1, source_target_pairs={{0,2},{1,3},{2,0},{3,1},{4,6},{5,7},{6,4},{7,5},{8,10},{9,11},{10,... | collective-permute-start | bytes 73736 | tf_op jit(solution)/shard_map/ppermute | solution.py:120

commit v9 on v8

--- a/solution.py
+++ b/solution.py
@@ -193,9 +193,8 @@
     line = lax.broadcasted_iota(jnp.int32, (modes, half), 0)
     wide = lax.broadcasted_iota(jnp.int32, (new, half), 1)
     unit = (wide == lax.broadcasted_iota(jnp.int32, (new, half), 0)).astype(jnp.float32)
-    sigma = jnp.concatenate(
-        [jnp.zeros((1, new), jnp.float32), sigma_ref[...], jnp.zeros((1, half - count), jnp.float32)], axis=1
-    )
+    sigma = jnp.concatenate([jnp.zeros((1, count), jnp.float32), sigma_ref[...]], axis=1)
+    early = jnp.concatenate([jnp.zeros((1, new), jnp.float32), sigma_ref[...], jnp.zeros((1, modes), jnp.float32)], axis=1)
 
     def at(place, x):
         above = [jnp.zeros((place, x.shape[1]), x.dtype)] if place else []
@@ -208,22 +207,23 @@
     sent = jnp.concatenate([upper, lower, lower], axis=0)
     late = lax.broadcasted_iota(jnp.int32, (new, half), 0) >= modes + modes // 2
     sent = jnp.where((wide >= new) & ((wide >= count) == late), sent, 0.0)
-    both = jnp.concatenate([twice, same], axis=1)
-    pair = dot(sent, jnp.concatenate([jnp.zeros((new, 2 * half), jnp.float32), both, both], axis=0))
-    joined_t, first_t = pair[:, :half], pair[:, half:]
+    above = jnp.zeros((new, half), jnp.float32)
+    joined_t = dot(sent, jnp.concatenate([above, twice, twice], axis=0))
+    pick = jnp.concatenate([above, same, same], axis=0).astype(jnp.bfloat16)
+    first_t = product_of(jnp.concatenate(pieces(sent), axis=1), jnp.concatenate([pick] * 3, axis=0))
     joined = dot(twice, at(0, first_t), NT)
-    joined_at = dot(first_t, at(new, twice), NT)
     rest = first_t - dot(joined_t, at(count, corr))
     residual = (
         snap_gram - dot(joined_t, at(0, first_t), NT) - dot(rest, at(0, joined_t), NT)
     )
-    corner = jnp.where(lane == new + line, sigma * sigma, 0.0) + dot(joined, at(new, joined), NT)
+    corner = jnp.where(lane == count + line, sigma * sigma, 0.0) + dot(joined, at(count, joined), NT)
+    scaling = jnp.where(lane == new + line, early * early, 0.0)
     bend = dot(joined, at(0, residual))
 
     step = jnp.concatenate(
         [
-            at(0, unit + joined_at) + at(new, joined + corner),
-            at(0, residual + joined_at) + at(new, bend + corner),
+            at(0, unit + joined_t) + at(count, joined + scaling + corner),
+            at(0, residual + joined_t) + at(count, bend + corner),
         ],
         axis=1,
     )
@@ -236,12 +236,11 @@
         frame_ref[...] = left
         return tuple(after)
 
-    start = (joined + corner, bend + corner)
+    start = (joined + scaling + corner, bend + corner)
     after, _ = lax.fori_loop(0, ITERS, iterate, start)
     left = frame_ref[...]
 
-    weights = (left - dot(left, at(0, joined_at)))[:, :count]
-    high, low_part = split(weights)
+    high, low_part = split(left[:, :count])
     left_side = jnp.concatenate(
         [jnp.concatenate([high, high], axis=1), jnp.concatenate([low_part, low_part], axis=1)], axis=0
     )

time: 29.1 us -> 29 us (level)
  no operation moved by 1% of the time
where the time goes in v9:
time: 29 us; the launch traced here: 28.8 us
  starting transfers between devices  10.5 us (36%)
  Pallas kernels  9.51 us (33%)
  waiting for transfers between devices  8.06 us (28%)
  between operations  0.66 us (2%)
    ppermute x5, starting transfers between devices, all_sum(): x = x + lax.ppermute(x, axis, [(i, i ^ bit) for i in range(size)])  10.5 us
    ppermute x5, waiting for transfers between devices, all_sum(): x = x + lax.ppermute(x, axis, [(i, i ^ bit) for i in range(size)])  8.06 us
    pallas_call x1, Pallas kernels, update(): pl.pallas_call(functools.partial(update_kernel, width), out_shape=(jax.Sh...  6.5 us
    pallas_call x1, Pallas kernels, gram(): pl.pallas_call(functools.partial(gram_kernel, 1.0 / total, width), out_sh...  3.01 us
  transfers between devices with their start and end apart: 5, of which 5 were waited for; matrix products, arithmetic and copies ran while one was open for 0% of the time, Pallas kernels for 0%

profile of v9, /device:TPU:0, one launch (start us, length us, event | category | flops | bytes accessed | tf_op | source)
XLA Modules:
  0.0 28.8 jit_solution(8636415704150567565)
XLA Ops:
  0.6 0.0 copy-start
  0.6 3.0 %gram.1 = f32[48,128]{1,0:T(8,128)S(1)} custom-call(f32[64,8192]{1,0:T(8,128)} %snap_ref.3, f32[32,8192]{1,0:T(8,128)} %basis_ref.3), custom_call_target="tpu_custom_call" | custom-call | tf_op jit(solution)/shard_map/gram/pallas_call | solution.py:99
  3.7 0.6 %collective-permute-start = (f32[48,128]{1,0:T(8,128)S(1)}, f32[48,128]{1,0:T(8,128)S(1)}, u32[]{:S(2)}, u32[]{:S(2)}) collective-permute-start(f32[48,128]{1,0:T(8,128)S(1)} %gram.1), channel_id=1, source_target_pairs={{0,16},{16,0},{1,17},{17,1},{2,18},{18,2},{3,19},{19,3},{4,20},{20... | collective-permute-start | bytes 73736 | tf_op jit(solution)/shard_map/ppermute | solution.py:120
  4.2 0.8 %collective-permute-done = f32[48,128]{1,0:T(8,128)S(1)} collective-permute-done((f32[48,128]{1,0:T(8,128)S(1)}, f32[48,128]{1,0:T(8,128)S(1)}, u32[]{:S(2)}, u32[]{:S(2)}) %collective-permute-start) | collective-permute-done | bytes 24608 | tf_op jit(solution)/shard_map/ppermute | solution.py:120
  5.1 2.8 %collective-permute-start.1 = (f32[48,128]{1,0:T(8,128)S(1)}, f32[48,128]{1,0:T(8,128)S(1)}, u32[]{:S(2)}, u32[]{:S(2)}) collective-permute-start(f32[48,128]{1,0:T(8,128)S(1)} %add.15), channel_id=1, source_target_pairs={{0,4},{4,0},{8,12},{12,8},{1,5},{5,1},{9,13},{13,9},{2,6},{6,2},{1... | collective-permute-start | bytes 73736 | tf_op jit(solution)/shard_map/ppermute | solution.py:120
  7.9 1.8 %collective-permute-done.1 = f32[48,128]{1,0:T(8,128)S(1)} collective-permute-done((f32[48,128]{1,0:T(8,128)S(1)}, f32[48,128]{1,0:T(8,128)S(1)}, u32[]{:S(2)}, u32[]{:S(2)}) %collective-permute-start.1) | collective-permute-done | bytes 24608 | tf_op jit(solution)/shard_map/ppermute | solution.py:120
  9.7 2.1 %collective-permute-start.2 = (f32[48,128]{1,0:T(8,128)S(1)}, f32[48,128]{1,0:T(8,128)S(1)}, u32[]{:S(2)}, u32[]{:S(2)}) collective-permute-start(f32[48,128]{1,0:T(8,128)S(1)} %add.16), channel_id=1, source_target_pairs={{0,8},{4,12},{8,0},{12,4},{1,9},{5,13},{9,1},{13,5},{2,10},{6,14},... | collective-permute-start | bytes 73736 | tf_op jit(solution)/shard_map/ppermute | solution.py:120
  11.8 1.8 %collective-permute-done.2 = f32[48,128]{1,0:T(8,128)S(1)} collective-permute-done((f32[48,128]{1,0:T(8,128)S(1)}, f32[48,128]{1,0:T(8,128)S(1)}, u32[]{:S(2)}, u32[]{:S(2)}) %collective-permute-start.2) | collective-permute-done | bytes 24608 | tf_op jit(solution)/shard_map/ppermute | solution.py:120
  13.6 2.1 %collective-permute-start.3 = (f32[48,128]{1,0:T(8,128)S(1)}, f32[48,128]{1,0:T(8,128)S(1)}, u32[]{:S(2)}, u32[]{:S(2)}) collective-permute-start(f32[48,128]{1,0:T(8,128)S(1)} %add.17), channel_id=1, source_target_pairs={{0,1},{1,0},{2,3},{3,2},{4,5},{5,4},{6,7},{7,6},{8,9},{9,8},{10,11... | collective-permute-start | bytes 73736 | tf_op jit(solution)/shard_map/ppermute | solution.py:120
  15.6 1.8 %collective-permute-done.3 = f32[48,128]{1,0:T(8,128)S(1)} collective-permute-done((f32[48,128]{1,0:T(8,128)S(1)}, f32[48,128]{1,0:T(8,128)S(1)}, u32[]{:S(2)}, u32[]{:S(2)}) %collective-permute-start.3) | collective-permute-done | bytes 24608 | tf_op jit(solution)/shard_map/ppermute | solution.py:120
  17.4 3.0 %collective-permute-start.4 = (f32[48,128]{1,0:T(8,128)S(1)}, f32[48,128]{1,0:T(8,128)S(1)}, u32[]{:S(2)}, u32[]{:S(2)}) collective-permute-start(f32[48,128]{1,0:T(8,128)S(1)} %add.18), channel_id=1, source_target_pairs={{0,2},{1,3},{2,0},{3,1},{4,6},{5,7},{6,4},{7,5},{8,10},{9,11},{10,... | collective-permute-start | bytes 73736 | tf_op jit(solution)/shard_map/ppermute | solution.py:120
  20.5 1.8 %collective-permute-done.4 = f32[48,128]{1,0:T(8,128)S(1)} collective-permute-done((f32[48,128]{1,0:T(8,128)S(1)}, f32[48,128]{1,0:T(8,128)S(1)}, u32[]{:S(2)}, u32[]{:S(2)}) %collective-permute-start.4) | collective-permute-done | bytes 24608 | tf_op jit(solution)/shard_map/ppermute | solution.py:120
  22.3 0.0 copy-done
  22.3 6.5 %update.1 = (f32[32,8192]{1,0:T(8,128)}, f32[1,32]{1,0:T(1,128)}) custom-call(f32[48,128]{1,0:T(8,128)S(1)} %add.19.sums_ref, f32[1,32]{1,0:T(1,128)S(1)} %bitcast.2, f32[64,8192]{1,0:T(8,128)} %snap_ref.3, f32[32,8192]{1,0:T(8,128)} %basis_ref.3), custom_call_target="tpu_custom_call" | custom-call | tf_op jit(solution)/shard_map/update/pallas_call | solution.py:271
  (5 shorter events, 0.0 us)
Async XLA Ops:
  0.6 21.7 %copy-start = (f32[32]{0:T(128)S(1)}, f32[32]{0:T(128)}, u32[]{:S(2)}) copy-start(f32[32]{0:T(128)} %param.4) | copy-start | bytes 388
  3.7 1.4 %collective-permute-start = (f32[48,128]{1,0:T(8,128)S(1)}, f32[48,128]{1,0:T(8,128)S(1)}, u32[]{:S(2)}, u32[]{:S(2)}) collective-permute-start(f32[48,128]{1,0:T(8,128)S(1)} %gram.1), channel_id=1, source_target_pairs={{0,16},{16,0},{1,17},{17,1},{2,18},{18,2},{3,19},{19,3},{4,20},{20... | collective-permute-start | bytes 73736 | tf_op jit(solution)/shard_map/ppermute | solution.py:120
  5.1 4.6 %collective-permute-start.1 = (f32[48,128]{1,0:T(8,128)S(1)}, f32[48,128]{1,0:T(8,128)S(1)}, u32[]{:S(2)}, u32[]{:S(2)}) collective-permute-start(f32[48,128]{1,0:T(8,128)S(1)} %add.15), channel_id=1, source_target_pairs={{0,4},{4,0},{8,12},{12,8},{1,5},{5,1},{9,13},{13,9},{2,6},{6,2},{1... | collective-permute-start | bytes 73736 | tf_op jit(solution)/shard_map/ppermute | solution.py:120
  9.7 3.9 %collective-permute-start.2 = (f32[48,128]{1,0:T(8,128)S(1)}, f32[48,128]{1,0:T(8,128)S(1)}, u32[]{:S(2)}, u32[]{:S(2)}) collective-permute-start(f32[48,128]{1,0:T(8,128)S(1)} %add.16), channel_id=1, source_target_pairs={{0,8},{4,12},{8,0},{12,4},{1,9},{5,13},{9,1},{13,5},{2,10},{6,14},... | collective-permute-start | bytes 73736 | tf_op jit(solution)/shard_map/ppermute | solution.py:120
  13.6 3.9 %collective-permute-start.3 = (f32[48,128]{1,0:T(8,128)S(1)}, f32[48,128]{1,0:T(8,128)S(1)}, u32[]{:S(2)}, u32[]{:S(2)}) collective-permute-start(f32[48,128]{1,0:T(8,128)S(1)} %add.17), channel_id=1, source_target_pairs={{0,1},{1,0},{2,3},{3,2},{4,5},{5,4},{6,7},{7,6},{8,9},{9,8},{10,11... | collective-permute-start | bytes 73736 | tf_op jit(solution)/shard_map/ppermute | solution.py:120
  17.4 4.8 %collective-permute-start.4 = (f32[48,128]{1,0:T(8,128)S(1)}, f32[48,128]{1,0:T(8,128)S(1)}, u32[]{:S(2)}, u32[]{:S(2)}) collective-permute-start(f32[48,128]{1,0:T(8,128)S(1)} %add.18), channel_id=1, source_target_pairs={{0,2},{1,3},{2,0},{3,1},{4,6},{5,7},{6,4},{7,5},{8,10},{9,11},{10,... | collective-permute-start | bytes 73736 | tf_op jit(solution)/shard_map/ppermute | solution.py:120

commit v10 on v9

--- a/solution.py
+++ b/solution.py
@@ -75,19 +75,24 @@
         piece = pl.ds(i * width, width)
         snap, basis = split(data_ref[:new, piece]), split(data_ref[new:, piece])
         rows = jnp.concatenate([snap[0], basis[0], snap[1], basis[1]], axis=0)
-        product = product_of(rows, rows, NT)
+        lanes = jnp.concatenate([snap[0], basis[0], basis[1], snap[1]], axis=0)
+        product = product_of(rows, lanes, NT)
         total = product if total is None else total + product
+    rows = (total[:count] + total[count:]) * scale
     sent = out_ref.shape[1]
-    rows = (total[:count] + total[count:]) * scale
-    rows = rows[:, :count] + rows[:, count:]
+    squares = rows[:, :sent] + jnp.concatenate([rows[:, sent:], jnp.zeros((count, sent - new), jnp.float32)], axis=1)
+    left = rows[:, :sent] + pltpu.roll(rows[:, :sent], sent - modes, 1)
+    right = rows[:, :sent] + pltpu.roll(rows[:, :sent], modes, 1)
     part = modes // 2
-    middle, last = rows[modes : modes + part], rows[modes + part : new]
-    out_ref[...] = jnp.concatenate(
-        [
-            jnp.concatenate([rows[:modes], rows[new:, new:]], axis=1),
-            jnp.concatenate([middle[:, modes:new], last[:, modes:new], middle[:, new:], last[:, new:]], axis=1),
-        ],
-        axis=0,
+    lane = lax.broadcasted_iota(jnp.int32, (modes, sent), 1)
+    out_ref[:modes] = jnp.where(lane < new, squares[:modes], jnp.where(lane < count, left[:modes], right[new:]))
+    lane = lane[:part]
+    middle, last = slice(modes, modes + part), slice(modes + part, new)
+    moved = pltpu.roll(squares[middle], sent - modes, 1)
+    out_ref[modes:] = jnp.where(
+        lane < modes,
+        moved,
+        jnp.where(lane < new, squares[last], jnp.where(lane < count, left[middle], right[last])),
     )
 
 

time: 29 us -> 28.9 us (level)
  no operation moved by 1% of the time
where the time goes in v10:
time: 28.9 us; the launch traced here: 28.7 us
  starting transfers between devices  10.5 us (36%)
  Pallas kernels  9.44 us (33%)
  waiting for transfers between devices  8.06 us (28%)
  between operations  0.66 us (2%)
    ppermute x5, starting transfers between devices, all_sum(): x = x + lax.ppermute(x, axis, [(i, i ^ bit) for i in range(size)])  10.5 us
    ppermute x5, waiting for transfers between devices, all_sum(): x = x + lax.ppermute(x, axis, [(i, i ^ bit) for i in range(size)])  8.06 us
    pallas_call x1, Pallas kernels, update(): pl.pallas_call(functools.partial(update_kernel, width), out_shape=(jax.Sh...  6.5 us
    pallas_call x1, Pallas kernels, gram(): pl.pallas_call(functools.partial(gram_kernel, 1.0 / total, width), out_sh...  2.94 us
  transfers between devices with their start and end apart: 5, of which 5 were waited for; matrix products, arithmetic and copies ran while one was open for 0% of the time, Pallas kernels for 0%

profile of v10, /device:TPU:0, one launch (start us, length us, event | category | flops | bytes accessed | tf_op | source)
XLA Modules:
  0.0 28.7 jit_solution(6584323706841705297)
XLA Ops:
  0.6 0.0 copy-start
  0.6 2.9 %gram.1 = f32[48,128]{1,0:T(8,128)S(1)} custom-call(f32[64,8192]{1,0:T(8,128)} %snap_ref.3, f32[32,8192]{1,0:T(8,128)} %basis_ref.3), custom_call_target="tpu_custom_call" | custom-call | tf_op jit(solution)/shard_map/gram/pallas_call | solution.py:104
  3.6 0.6 %collective-permute-start = (f32[48,128]{1,0:T(8,128)S(1)}, f32[48,128]{1,0:T(8,128)S(1)}, u32[]{:S(2)}, u32[]{:S(2)}) collective-permute-start(f32[48,128]{1,0:T(8,128)S(1)} %gram.1), channel_id=1, source_target_pairs={{0,16},{16,0},{1,17},{17,1},{2,18},{18,2},{3,19},{19,3},{4,20},{20... | collective-permute-start | bytes 73736 | tf_op jit(solution)/shard_map/ppermute | solution.py:125
  4.2 0.8 %collective-permute-done = f32[48,128]{1,0:T(8,128)S(1)} collective-permute-done((f32[48,128]{1,0:T(8,128)S(1)}, f32[48,128]{1,0:T(8,128)S(1)}, u32[]{:S(2)}, u32[]{:S(2)}) %collective-permute-start) | collective-permute-done | bytes 24608 | tf_op jit(solution)/shard_map/ppermute | solution.py:125
  5.0 2.8 %collective-permute-start.1 = (f32[48,128]{1,0:T(8,128)S(1)}, f32[48,128]{1,0:T(8,128)S(1)}, u32[]{:S(2)}, u32[]{:S(2)}) collective-permute-start(f32[48,128]{1,0:T(8,128)S(1)} %add.15), channel_id=1, source_target_pairs={{0,4},{4,0},{8,12},{12,8},{1,5},{5,1},{9,13},{13,9},{2,6},{6,2},{1... | collective-permute-start | bytes 73736 | tf_op jit(solution)/shard_map/ppermute | solution.py:125
  7.8 1.8 %collective-permute-done.1 = f32[48,128]{1,0:T(8,128)S(1)} collective-permute-done((f32[48,128]{1,0:T(8,128)S(1)}, f32[48,128]{1,0:T(8,128)S(1)}, u32[]{:S(2)}, u32[]{:S(2)}) %collective-permute-start.1) | collective-permute-done | bytes 24608 | tf_op jit(solution)/shard_map/ppermute | solution.py:125
  9.6 2.0 %collective-permute-start.2 = (f32[48,128]{1,0:T(8,128)S(1)}, f32[48,128]{1,0:T(8,128)S(1)}, u32[]{:S(2)}, u32[]{:S(2)}) collective-permute-start(f32[48,128]{1,0:T(8,128)S(1)} %add.16), channel_id=1, source_target_pairs={{0,8},{4,12},{8,0},{12,4},{1,9},{5,13},{9,1},{13,5},{2,10},{6,14},... | collective-permute-start | bytes 73736 | tf_op jit(solution)/shard_map/ppermute | solution.py:125
  11.7 1.8 %collective-permute-done.2 = f32[48,128]{1,0:T(8,128)S(1)} collective-permute-done((f32[48,128]{1,0:T(8,128)S(1)}, f32[48,128]{1,0:T(8,128)S(1)}, u32[]{:S(2)}, u32[]{:S(2)}) %collective-permute-start.2) | collective-permute-done | bytes 24608 | tf_op jit(solution)/shard_map/ppermute | solution.py:125
  13.5 2.1 %collective-permute-start.3 = (f32[48,128]{1,0:T(8,128)S(1)}, f32[48,128]{1,0:T(8,128)S(1)}, u32[]{:S(2)}, u32[]{:S(2)}) collective-permute-start(f32[48,128]{1,0:T(8,128)S(1)} %add.17), channel_id=1, source_target_pairs={{0,1},{1,0},{2,3},{3,2},{4,5},{5,4},{6,7},{7,6},{8,9},{9,8},{10,11... | collective-permute-start | bytes 73736 | tf_op jit(solution)/shard_map/ppermute | solution.py:125
  15.6 1.8 %collective-permute-done.3 = f32[48,128]{1,0:T(8,128)S(1)} collective-permute-done((f32[48,128]{1,0:T(8,128)S(1)}, f32[48,128]{1,0:T(8,128)S(1)}, u32[]{:S(2)}, u32[]{:S(2)}) %collective-permute-start.3) | collective-permute-done | bytes 24608 | tf_op jit(solution)/shard_map/ppermute | solution.py:125
  17.4 3.0 %collective-permute-start.4 = (f32[48,128]{1,0:T(8,128)S(1)}, f32[48,128]{1,0:T(8,128)S(1)}, u32[]{:S(2)}, u32[]{:S(2)}) collective-permute-start(f32[48,128]{1,0:T(8,128)S(1)} %add.18), channel_id=1, source_target_pairs={{0,2},{1,3},{2,0},{3,1},{4,6},{5,7},{6,4},{7,5},{8,10},{9,11},{10,... | collective-permute-start | bytes 73736 | tf_op jit(solution)/shard_map/ppermute | solution.py:125
  20.4 1.8 %collective-permute-done.4 = f32[48,128]{1,0:T(8,128)S(1)} collective-permute-done((f32[48,128]{1,0:T(8,128)S(1)}, f32[48,128]{1,0:T(8,128)S(1)}, u32[]{:S(2)}, u32[]{:S(2)}) %collective-permute-start.4) | collective-permute-done | bytes 24608 | tf_op jit(solution)/shard_map/ppermute | solution.py:125
  22.2 0.0 copy-done
  22.2 6.5 %update.1 = (f32[32,8192]{1,0:T(8,128)}, f32[1,32]{1,0:T(1,128)}) custom-call(f32[48,128]{1,0:T(8,128)S(1)} %add.19.sums_ref, f32[1,32]{1,0:T(1,128)S(1)} %bitcast.2, f32[64,8192]{1,0:T(8,128)} %snap_ref.3, f32[32,8192]{1,0:T(8,128)} %basis_ref.3), custom_call_target="tpu_custom_call" | custom-call | tf_op jit(solution)/shard_map/update/pallas_call | solution.py:276
  (5 shorter events, 0.0 us)
Async XLA Ops:
  0.6 21.6 %copy-start = (f32[32]{0:T(128)S(1)}, f32[32]{0:T(128)}, u32[]{:S(2)}) copy-start(f32[32]{0:T(128)} %param.4) | copy-start | bytes 388
  3.6 1.4 %collective-permute-start = (f32[48,128]{1,0:T(8,128)S(1)}, f32[48,128]{1,0:T(8,128)S(1)}, u32[]{:S(2)}, u32[]{:S(2)}) collective-permute-start(f32[48,128]{1,0:T(8,128)S(1)} %gram.1), channel_id=1, source_target_pairs={{0,16},{16,0},{1,17},{17,1},{2,18},{18,2},{3,19},{19,3},{4,20},{20... | collective-permute-start | bytes 73736 | tf_op jit(solution)/shard_map/ppermute | solution.py:125
  5.0 4.6 %collective-permute-start.1 = (f32[48,128]{1,0:T(8,128)S(1)}, f32[48,128]{1,0:T(8,128)S(1)}, u32[]{:S(2)}, u32[]{:S(2)}) collective-permute-start(f32[48,128]{1,0:T(8,128)S(1)} %add.15), channel_id=1, source_target_pairs={{0,4},{4,0},{8,12},{12,8},{1,5},{5,1},{9,13},{13,9},{2,6},{6,2},{1... | collective-permute-start | bytes 73736 | tf_op jit(solution)/shard_map/ppermute | solution.py:125
  9.6 3.9 %collective-permute-start.2 = (f32[48,128]{1,0:T(8,128)S(1)}, f32[48,128]{1,0:T(8,128)S(1)}, u32[]{:S(2)}, u32[]{:S(2)}) collective-permute-start(f32[48,128]{1,0:T(8,128)S(1)} %add.16), channel_id=1, source_target_pairs={{0,8},{4,12},{8,0},{12,4},{1,9},{5,13},{9,1},{13,5},{2,10},{6,14},... | collective-permute-start | bytes 73736 | tf_op jit(solution)/shard_map/ppermute | solution.py:125
  13.5 3.9 %collective-permute-start.3 = (f32[48,128]{1,0:T(8,128)S(1)}, f32[48,128]{1,0:T(8,128)S(1)}, u32[]{:S(2)}, u32[]{:S(2)}) collective-permute-start(f32[48,128]{1,0:T(8,128)S(1)} %add.17), channel_id=1, source_target_pairs={{0,1},{1,0},{2,3},{3,2},{4,5},{5,4},{6,7},{7,6},{8,9},{9,8},{10,11... | collective-permute-start | bytes 73736 | tf_op jit(solution)/shard_map/ppermute | solution.py:125
  17.4 4.8 %collective-permute-start.4 = (f32[48,128]{1,0:T(8,128)S(1)}, f32[48,128]{1,0:T(8,128)S(1)}, u32[]{:S(2)}, u32[]{:S(2)}) collective-permute-start(f32[48,128]{1,0:T(8,128)S(1)} %add.18), channel_id=1, source_target_pairs={{0,2},{1,3},{2,0},{3,1},{4,6},{5,7},{6,4},{7,5},{8,10},{9,11},{10,... | collective-permute-start | bytes 73736 | tf_op jit(solution)/shard_map/ppermute | solution.py:125
